TPU v7x, 32 devices: a whole 2x2x4 slice. The times are simulated.
32 devices in a mesh: batch: 8 (over y, x, core), mp: 4 (over z).
Axes of the slice: x: 2, y: 2, z: 4, core: 2. Of those that a mesh axis runs over, the one named last changes fastest.
Arguments:
- token_ids: int32 [8, 1536], P('batch'), may hold values from 0 to 30527
- segment_ids: int32 [8, 1536], P('batch'), may hold values from 0 to 8, never falling along the last dimension, each value on 1 to 1024 neighbouring positions
- row_of: int32 [30528], replicated, may hold values from 0 to 30527, each once
- query_count: int32 [1], replicated, may hold values from 16 to 32
- table: float32 [30528, 768], P('batch'), may hold values from -8 to 8
- qkv_weight: float32 [768, 3, 768], P('batch', None, 'mp'), may hold values from -0.21875 to 0.21875
- out_weight: float32 [768, 768], P('mp', 'batch'), may hold values from -0.875 to 0.875
- gate_up_weight: float32 [768, 2, 3072], P('batch', None, 'mp'), may hold values from -0.21875 to 0.21875
- down_weight: float32 [3072, 768], P('mp', 'batch'), may hold values from -0.109375 to 0.109375
- gains: float32 [2, 768], P(None, 'batch'), may hold values from 0.3 to 2.5
- table_m: float32 [30528, 768], P('batch'), may hold values from -0.0009765625 to 0.0009765625
- qkv_m: float32 [768, 3, 768], P('batch', None, 'mp'), may hold values from -0.0009765625 to 0.0009765625
- out_m: float32 [768, 768], P('mp', 'batch'), may hold values from -0.0009765625 to 0.0009765625
- gate_up_m: float32 [768, 2, 3072], P('batch', None, 'mp'), may hold values from -0.0009765625 to 0.0009765625
- down_m: float32 [3072, 768], P('mp', 'batch'), may hold values from -0.0009765625 to 0.0009765625
- gains_m: float32 [2, 768], P(None, 'batch'), may hold values from -0.0009765625 to 0.0009765625
- table_v: float32 [30528, 768], P('batch'), may hold values from 3.040972e-08 to 1.2163888e-07
- qkv_v: float32 [768, 3, 768], P('batch', None, 'mp'), may hold values from 3.040972e-08 to 1.2163888e-07
- out_v: float32 [768, 768], P('mp', 'batch'), may hold values from 3.040972e-08 to 1.2163888e-07
- gate_up_v: float32 [768, 2, 3072], P('batch', None, 'mp'), may hold values from 3.040972e-08 to 1.2163888e-07
- down_v: float32 [3072, 768], P('mp', 'batch'), may hold values from 3.040972e-08 to 1.2163888e-07
- gains_v: float32 [2, 768], P(None, 'batch'), may hold values from 3.040972e-08 to 1.2163888e-07
Outputs:
- loss: float32 [1], replicated
- grad_norm: float32 [1], replicated
- new_table: float32 [30528, 768], P('batch')
- new_qkv_weight: float32 [768, 3, 768], P('batch', None, 'mp')
- new_out_weight: float32 [768, 768], P('mp', 'batch')
- new_gate_up_weight: float32 [768, 2, 3072], P('batch', None, 'mp')
- new_down_weight: float32 [3072, 768], P('mp', 'batch')
- new_gains: float32 [2, 768], P(None, 'batch')
- clipped_table_grad: float32 [30528, 768], P('batch')
- new_qkv_m: float32 [768, 3, 768], P('batch', None, 'mp')
- new_out_m: float32 [768, 768], P('mp', 'batch')
- new_gate_up_m: float32 [768, 2, 3072], P('batch', None, 'mp')
- new_down_m: float32 [3072, 768], P('mp', 'batch')
- new_gains_m: float32 [2, 768], P(None, 'batch')
- new_table_v: float32 [30528, 768], P('batch')
- new_qkv_v: float32 [768, 3, 768], P('batch', None, 'mp')
- new_out_v: float32 [768, 768], P('mp', 'batch')
- new_gate_up_v: float32 [768, 2, 3072], P('batch', None, 'mp')
- new_down_v: float32 [3072, 768], P('mp', 'batch')
- new_gains_v: float32 [2, 768], P(None, 'batch')
Inputs may be any that keep to these rules, and one draw needn't show every extreme that they name: `segment_ids`: in each row the ids never fall, every id 0 to 8 appears, id 8 marks padding, each segment has 1 to 1024 tokens and one has exactly 1024. A permutation: token t's embedding is table row row_of[t]. The first query_count queries count.
All inputs are finite; a program needn't handle non-finite values.
Results may differ from a plain program's by a relative error of at most 0.0075.
The roundings to bfloat16 on the way count: a program that leaves them out, or rounds other values in their place, can miss the bound.
Values may be sent and summed in bfloat16 or wider, within the bound.
A program may use at most 320 MiB of HBM per device.

v0:
```python
from functools import partial

import jax
import jax.numpy as jnp
from jax import lax
from jax.sharding import PartitionSpec as P

D = 768
HEAD_DIM = 64
SEGS = 8


peak_affinity = lax.Precision.HIGHEST
sharpness_divisor = 0.05
clip_limit = 1.0
step_number = 3.0
rates = (0.3, 0.02, 0.02, 0.02, 0.02, 0.3)
negative = -1e30


def positions(segment_row, segment_count):
    labels = jnp.arange(segment_count + 1, dtype=jnp.int32)
    member = (segment_row[:, None] == labels[None, :]).astype(jnp.int32)
    counts = jnp.sum(member, 0)
    starts = jnp.cumsum(counts) - counts
    first_index = jnp.sum(member * starts[None, :], 1)
    return (jnp.arange(segment_row.shape[0], dtype=jnp.int32) - first_index).astype(jnp.float32)


def rotate(values, places):
    half_dim = values.shape[-1] // 2
    freqs = jnp.power(1000.0, -2.0 * jnp.arange(half_dim, dtype=jnp.float32) / values.shape[-1])
    angles = places[:, None] * freqs[None, :]
    cosine = jnp.cos(angles)[:, None, :]
    sine = jnp.sin(angles)[:, None, :]
    former = values[..., :half_dim]
    latter = values[..., half_dim:]
    return jnp.concatenate([former * cosine - latter * sine, latter * cosine + former * sine], -1)


def layer_norm(values, gain):
    centred = values - jnp.mean(values, -1, keepdims=True)
    spread = jnp.mean(centred * centred, -1, keepdims=True)
    return centred * lax.rsqrt(spread + 1e-05) * gain


def swiglu(gate_up):
    return jax.nn.silu(gate_up[:, 0]) * gate_up[:, 1]


def contract(left, right, left_dim, right_dim):
    return lax.dot_general(
        left, right, (((left_dim,), (right_dim,)), ((), ())), preferred_element_type=jnp.float32
    )


def pool_rows(hidden, segment_ids):
    rows_dev, length = segment_ids.shape
    labels = jnp.arange(SEGS, dtype=jnp.int32)
    member = (segment_ids[:, None, :] == labels[None, :, None]).astype(jnp.float32)
    sums = jnp.einsum(
        "rsl,rld->rsd", member, hidden.reshape(rows_dev, length, -1), precision=peak_affinity
    )
    pooled = (sums / jnp.sum(member, -1, keepdims=True)).reshape(rows_dev * SEGS, -1)
    return pooled * lax.rsqrt(jnp.sum(pooled * pooled, -1, keepdims=True) + 1e-06)


def block_scores(query_block, key_row, segment_block, segment_row):
    scores = jnp.einsum(
        "qhd,khd->hqk", query_block, key_row, preferred_element_type=jnp.float32
    ) * HEAD_DIM ** (-0.5)
    same = segment_block[:, None] == segment_row[None, :]
    return jnp.where(same[None], scores, negative)


def attend(query, keys, values, segment_ids, width):
    rows_dev, length = segment_ids.shape
    per_row = length // width
    flat_segments = segment_ids.reshape(-1)

    def one_block(block):
        row_index = block // per_row
        query_block = lax.dynamic_slice_in_dim(query, block * width, width, 0)
        segment_block = lax.dynamic_slice_in_dim(flat_segments, block * width, width, 0)
        scores = block_scores(query_block, keys[row_index], segment_block, segment_ids[row_index])
        peak_score = jnp.max(scores, -1, keepdims=True)
        weights = jnp.exp(scores - peak_score)
        totals = jnp.sum(weights, -1, keepdims=True)
        probs = (weights / totals).astype(jnp.bfloat16)
        output = jnp.einsum(
            "hqk,khd->qhd", probs, values[row_index], preferred_element_type=jnp.float32
        )
        return (output, (peak_score + jnp.log(totals))[..., 0])

    outputs, log_totals = lax.map(one_block, jnp.arange(rows_dev * per_row, dtype=jnp.int32))
    return (outputs.reshape((rows_dev * length,) + outputs.shape[2:]), log_totals)


def attend_back(query, keys, values, segment_ids, log_totals, grad_out, width):
    rows_dev, length = segment_ids.shape
    per_row = length // width
    flat_segments = segment_ids.reshape(-1)
    factor = HEAD_DIM ** (-0.5)

    def one_block(carry, block):
        grad_keys, grad_values = carry
        row_index = block // per_row
        query_block = lax.dynamic_slice_in_dim(query, block * width, width, 0)
        segment_block = lax.dynamic_slice_in_dim(flat_segments, block * width, width, 0)
        grad_block = lax.dynamic_slice_in_dim(grad_out, block * width, width, 0)
        scores = block_scores(query_block, keys[row_index], segment_block, segment_ids[row_index])
        probs = jnp.exp(scores - log_totals[block][..., None])
        grad_probs = jnp.einsum(
            "qhd,khd->hqk", grad_block, values[row_index], preferred_element_type=jnp.float32
        )
        inner = jnp.sum(probs * grad_probs, -1, keepdims=True)
        grad_scores = (probs * (grad_probs - inner)).astype(jnp.bfloat16)
        grad_query = (
            jnp.einsum(
                "hqk,khd->qhd", grad_scores, keys[row_index], preferred_element_type=jnp.float32
            )
            * factor
        )
        key_term = (
            jnp.einsum("hqk,qhd->khd", grad_scores, query_block, preferred_element_type=jnp.float32)
            * factor
        )
        value_term = jnp.einsum(
            "hqk,qhd->khd",
            probs.astype(jnp.bfloat16),
            grad_block,
            preferred_element_type=jnp.float32,
        )
        return (
            (grad_keys.at[row_index].add(key_term), grad_values.at[row_index].add(value_term)),
            grad_query,
        )

    zeros = jnp.zeros(keys.shape, jnp.float32)
    (grad_keys, grad_values), grad_query = lax.scan(
        one_block, (zeros, zeros), jnp.arange(rows_dev * per_row, dtype=jnp.int32)
    )
    return (grad_query.reshape((rows_dev * length,) + grad_query.shape[2:]), grad_keys, grad_values)


def adam_update(weight, grad, first, second, rate):
    first = 0.5 * first + 0.5 * grad
    second = 0.5 * second + 0.5 * grad * grad
    correction = 1.0 - 0.5**step_number
    weight = weight - rate * (
        first / correction / (jnp.sqrt(second / correction) + 1e-08) + 0.01 * weight
    )
    return (weight, first, second)


def local(
    token_ids,
    segment_ids,
    row_of,
    query_count,
    table,
    qkv_weight,
    out_weight,
    gate_up_weight,
    down_weight,
    gains,
    table_m,
    qkv_m,
    out_m,
    gate_up_m,
    down_m,
    gains_m,
    table_v,
    qkv_v,
    out_v,
    gate_up_v,
    down_v,
    gains_v,
):
    local_width = table.shape[1] // lax.axis_size("mp")
    column = lax.axis_index("mp") * local_width
    table_cols = lax.dynamic_slice_in_dim(table, column, local_width, 1)
    low_table, w_qkv, w_out, w_gu, w_down, gain_low = (
        lax.all_gather(table_cols.astype(jnp.bfloat16), "batch", axis=0, tiled=True),
        lax.all_gather(qkv_weight.astype(jnp.bfloat16), "batch", axis=0, tiled=True),
        lax.all_gather(out_weight.astype(jnp.bfloat16), "batch", axis=1, tiled=True),
        lax.all_gather(gate_up_weight.astype(jnp.bfloat16), "batch", axis=0, tiled=True),
        lax.all_gather(down_weight.astype(jnp.bfloat16), "batch", axis=1, tiled=True),
        lax.all_gather(gains.astype(jnp.bfloat16), "batch", axis=1, tiled=True),
    )
    gain = gain_low.astype(jnp.float32)
    rows_dev, length = token_ids.shape
    tokens = rows_dev * length
    width = min(512, length)
    heads_local = w_qkv.shape[2] // HEAD_DIM
    ff_local = w_gu.shape[2]
    table_rows = row_of[token_ids.reshape(-1)]
    x_zero = lax.all_gather(low_table[table_rows], "mp", axis=1, tiled=True)
    places = jax.vmap(partial(positions, segment_count=SEGS))(segment_ids).reshape(-1)
    qkv = jnp.dot(x_zero, w_qkv.reshape(D, -1), preferred_element_type=jnp.float32).reshape(
        tokens, 3, heads_local, HEAD_DIM
    )
    query = rotate(qkv[:, 0], places).astype(jnp.bfloat16)
    keys = (
        rotate(qkv[:, 1], places)
        .astype(jnp.bfloat16)
        .reshape(rows_dev, length, heads_local, HEAD_DIM)
    )
    values = qkv[:, 2].astype(jnp.bfloat16).reshape(rows_dev, length, heads_local, HEAD_DIM)
    attended, log_totals = attend(query, keys, values, segment_ids, width)
    attended_low = attended.reshape(tokens, -1).astype(jnp.bfloat16)
    attn_term = jnp.dot(attended_low, w_out, preferred_element_type=jnp.float32)
    attn = lax.psum(attn_term, "mp")
    hidden_one, first_back = jax.vjp(layer_norm, x_zero.astype(jnp.float32) + attn, gain[0])
    hidden_low = hidden_one.astype(jnp.bfloat16)
    gate_up = jnp.dot(hidden_low, w_gu.reshape(D, -1), preferred_element_type=jnp.float32).reshape(
        tokens, 2, ff_local
    )
    active, swiglu_back = jax.vjp(swiglu, gate_up)
    active_low = active.astype(jnp.bfloat16)
    mlp = lax.psum(jnp.dot(active_low, w_down, preferred_element_type=jnp.float32), "mp")
    hidden_two, second_back = jax.vjp(layer_norm, hidden_one + mlp, gain[1])
    embed, pool_back = jax.vjp(lambda hidden: pool_rows(hidden, segment_ids), hidden_two)
    batch_index = lax.axis_index("batch")
    half_count = lax.axis_size("batch") // 2
    texts = embed.shape[0]
    queries_all = half_count * texts
    everyone = lax.all_gather(embed, "batch", axis=0, tiled=True)
    question_vectors = everyone[:queries_all]
    passage_vectors = everyone[queries_all:]
    limit = query_count[0].astype(jnp.float32)
    labels = jnp.arange(queries_all, dtype=jnp.int32)
    weight_rows = (labels < query_count[0]).astype(jnp.float32) / limit
    affinity_scores = (
        jnp.dot(question_vectors, passage_vectors.T, precision=peak_affinity) / sharpness_divisor
    )
    target = (labels[:, None] == labels[None, :]).astype(jnp.float32)
    loss_value = jnp.sum(
        weight_rows
        * (jax.nn.logsumexp(affinity_scores, -1) - jnp.sum(affinity_scores * target, -1))
    )
    affinity_derivative = (jax.nn.softmax(affinity_scores, -1) - target) * weight_rows[:, None]
    grad_all = jnp.concatenate(
        [
            jnp.dot(affinity_derivative, passage_vectors, precision=peak_affinity)
            / sharpness_divisor,
            jnp.dot(affinity_derivative.T, question_vectors, precision=peak_affinity)
            / sharpness_divisor,
        ],
        0,
    )
    grad_embed = lax.dynamic_slice_in_dim(grad_all, batch_index * texts, texts, 0)
    (grad_two,) = pool_back(grad_embed)
    grad_second, grad_gain_two = second_back(grad_two)
    grad_mlp_low = grad_second.astype(jnp.bfloat16)
    grad_active = contract(grad_mlp_low, w_down, 1, 1)
    grad_down = contract(active_low, grad_mlp_low, 0, 0)
    (grad_gate_up,) = swiglu_back(grad_active)
    grad_gu_low = grad_gate_up.reshape(tokens, -1).astype(jnp.bfloat16)
    back_term = contract(grad_gu_low, w_gu.reshape(D, -1), 1, 1)
    grad_one = grad_second + lax.psum(back_term, "mp")
    grad_first, grad_gain_one = first_back(grad_one)
    grad_gu = contract(hidden_low, grad_gu_low, 0, 0)
    grad_attn_low = grad_first.astype(jnp.bfloat16)
    grad_attended = contract(grad_attn_low, w_out, 1, 1).astype(jnp.bfloat16)
    grad_out = contract(attended_low, grad_attn_low, 0, 0)
    grad_query, grad_keys, grad_values = attend_back(
        query,
        keys,
        values,
        segment_ids,
        log_totals,
        grad_attended.reshape(tokens, heads_local, HEAD_DIM),
        width,
    )
    _, rotate_back = jax.vjp(lambda inputs: rotate(inputs, places), qkv[:, 0])
    (grad_query_raw,) = rotate_back(grad_query)
    (grad_key_raw,) = rotate_back(grad_keys.reshape(tokens, heads_local, HEAD_DIM))
    grad_qkv_low = (
        jnp.stack(
            [grad_query_raw, grad_key_raw, grad_values.reshape(tokens, heads_local, HEAD_DIM)], 1
        )
        .reshape(tokens, -1)
        .astype(jnp.bfloat16)
    )
    grad_zero = grad_first + lax.psum(contract(grad_qkv_low, w_qkv.reshape(D, -1), 1, 1), "mp")
    grad_qkv = contract(x_zero, grad_qkv_low, 0, 0)
    grad_table = (
        jnp.zeros((low_table.shape[0], local_width), jnp.float32)
        .at[table_rows]
        .add(lax.dynamic_slice_in_dim(grad_zero, column, local_width, 1))
    )
    grad_gains = jnp.stack([grad_gain_one, grad_gain_two], 0)
    reduced = (
        lax.psum_scatter(grad_table, "batch", scatter_dimension=0, tiled=True),
        lax.psum_scatter(grad_qkv.reshape(D, 3, -1), "batch", scatter_dimension=0, tiled=True),
        lax.psum_scatter(grad_out, "batch", scatter_dimension=1, tiled=True),
        lax.psum_scatter(grad_gu.reshape(D, 2, -1), "batch", scatter_dimension=0, tiled=True),
        lax.psum_scatter(grad_down, "batch", scatter_dimension=1, tiled=True),
        lax.psum_scatter(grad_gains, "batch", scatter_dimension=1, tiled=True),
    )
    squares = sum((jnp.sum(part * part) for part in reduced[:5])) + jnp.sum(
        reduced[5] * reduced[5]
    ) / lax.axis_size("mp")
    table_full = lax.all_gather(reduced[0], "mp", axis=1, tiled=True)
    total_squares = lax.psum(squares, ("batch", "mp"))
    grad_norm = jnp.sqrt(total_squares)
    scale = clip_limit / jnp.maximum(grad_norm, clip_limit)
    olds = (table, qkv_weight, out_weight, gate_up_weight, down_weight, gains)
    grads_all = (table_full,) + tuple(reduced[1:])
    firsts = (table_m, qkv_m, out_m, gate_up_m, down_m, gains_m)
    seconds = (table_v, qkv_v, out_v, gate_up_v, down_v, gains_v)
    updated = [
        adam_update(weight_old, grad_part * scale, first_old, second_old, rate)
        for weight_old, grad_part, first_old, second_old, rate in zip(
            olds, grads_all, firsts, seconds, rates
        )
    ]
    clipped_table = table_full * scale
    loss = loss_value.reshape(1)
    return (
        loss,
        grad_norm.reshape(1),
        updated[0][0],
        updated[1][0],
        updated[2][0],
        updated[3][0],
        updated[4][0],
        updated[5][0],
        clipped_table,
        updated[1][1],
        updated[2][1],
        updated[3][1],
        updated[4][1],
        updated[5][1],
        updated[0][2],
        updated[1][2],
        updated[2][2],
        updated[3][2],
        updated[4][2],
        updated[5][2],
    )


def solution(mesh):
    placed = (
        P("batch", None),
        P("batch", None),
        P(),
        P(),
        P("batch", None),
        P("batch", None, "mp"),
        P("mp", "batch"),
        P("batch", None, "mp"),
        P("mp", "batch"),
        P(None, "batch"),
        P("batch", None),
        P("batch", None, "mp"),
        P("mp", "batch"),
        P("batch", None, "mp"),
        P("mp", "batch"),
        P(None, "batch"),
        P("batch", None),
        P("batch", None, "mp"),
        P("mp", "batch"),
        P("batch", None, "mp"),
        P("mp", "batch"),
        P(None, "batch"),
    )
    return jax.shard_map(
        local,
        mesh=mesh,
        in_specs=placed,
        out_specs=(
            P(),
            P(),
            P("batch", None),
            P("batch", None, "mp"),
            P("mp", "batch"),
            P("batch", None, "mp"),
            P("mp", "batch"),
            P(None, "batch"),
            P("batch", None),
            P("batch", None, "mp"),
            P("mp", "batch"),
            P("batch", None, "mp"),
            P("mp", "batch"),
            P(None, "batch"),
            P("batch", None),
            P("batch", None, "mp"),
            P("mp", "batch"),
            P("batch", None, "mp"),
            P("mp", "batch"),
            P(None, "batch"),
        ),
        check_vma=False,
    )
```

profile of v0, /device:TPU:0, one launch (start us, length us, event | category | flops | bytes accessed | tf_op | source)
XLA Modules:
  0.0 1895.7 jit_solution(3074774490312549609)
XLA Ops:
  7.3 12.4 copy.141
  22.9 8.4 gather_fusion
  31.4 63.1 %all-gather.17.cloned.1.call-done = bf16[8,3816,192]{1,2,0:T(8,128)(2,1)} async-done(((bf16[1,3816,192]{1,2,0:T(8,128)(2,1)}), bf16[8,3816,192]{1,2,0:T(8,128)(2,1)}) %all-gather.17.cloned.1.call-update) | async-done | bytes 11722768 | tf_op jit(solution)/shard_map/all_gather | solution.py:184
  94.5 18.1 copy.142
  112.6 11.2 gather_fusion.1
  126.6 13.2 all_gather.29
  141.9 8.8 all_gather.30
  151.5 24.0 %all-gather.15.cloned.1.call-done = bf16[1536,768]{0,1:T(8,128)(2,1)} async-done(((bf16[1536,192]{0,1:T(8,128)(2,1)}), bf16[1536,768]{0,1:T(8,128)(2,1)}) %all-gather.15.cloned.1.call-update) | async-done | bytes 2359312 | tf_op jit(solution)/shard_map/all_gather | solution.py:198
  179.8 33.9 %while.31 = (s32[]{:T(128)}, bf16[3,512,3,64]{1,3,2,0:T(8,128)(2,1)}, f32[3,3,512]{2,1,0:T(4,128)S(1)}, s32[3]{0:T(128)S(1)}, s32[1536]{0:T(1024)S(1)}, /*index=...) while((s32[]{:T(128)}, ...), condition=%wide.region_6.7_spmd, body=%wide.region_3.6_spmd.sunk | while | flops 633076224 | bytes 38029568 | solution.py:95
  219.3 8.9 all-gather.2
  232.6 156.7 %all-reduce.11.cloned.1.call-done = f32[1536,768]{0,1:T(8,128)} async-done(((f32[1536,768]{0,1:T(8,128)}), f32[1536,768]{0,1:T(8,128)}) %all-reduce.11.cloned.1.call-update) | async-done | bytes 4718608 | tf_op jit(solution)/shard_map/psum | solution.py:213
  407.1 7.7 all-gather.11.cloned.1.call-done
  414.8 6.2 fusion.123
  421.9 171.2 %all-reduce.13.cloned.1.call-done = f32[1536,768]{0,1:T(8,128)} async-done(((f32[1536,768]{0,1:T(8,128)}), f32[1536,768]{0,1:T(8,128)}) %all-reduce.13.cloned.1.call-update) | async-done | bytes 4718608 | tf_op jit(solution)/shard_map/psum | solution.py:221
  601.2 9.7 all_gather.34
  625.5 7.9 convolution_bitcast_fusion
  633.6 169.9 %all-reduce.15.cloned.1.call-done = f32[1536,768]{0,1:T(8,128)} async-done(((f32[1536,768]{0,1:T(8,128)}), f32[1536,768]{0,1:T(8,128)}) %all-reduce.15.cloned.1.call-update) | async-done | bytes 4718608 | tf_op jit(solution)/shard_map/psum | solution.py:261
  803.6 6.2 multiply_reduce_fusion.2
  821.5 161.7 %while.32 = (s32[]{:T(128)}, f32[1,1536,3,64]{1,3,2,0:T(8,128)}, f32[1,1536,3,64]{1,3,2,0:T(8,128)S(1)}, f32[3,512,3,64]{1,0,3,2:T(4,128)}, s32[3]{0:T(128)S(1)}...) while((s32[]{:T(128)}, f32[1,1536,3,64]{1,3,2,0:T(8,128)}, ...), condition=%wide.region_29.30_spmd.clone, body=%wide.region_26.29_spmd.clone.sunk | while | flops 1534130688 | bytes 86367704 | solution.py:140
  822.8 6.1 fusion.167
  831.5 8.1 multiply_reduce_fusion.16
  839.5 9.4 multiply_convert_fusion.4
  853.2 8.6 dynamic_update_slice.22
  876.5 6.1 fusion.167
  885.2 8.1 multiply_reduce_fusion.16
  893.2 9.4 multiply_convert_fusion.4
  906.9 8.6 dynamic_update_slice.22
  939.2 8.1 multiply_reduce_fusion.16
  947.3 9.4 multiply_convert_fusion.4
  960.9 8.6 dynamic_update_slice.22
  993.2 171.1 %all-reduce.17.cloned.1.call-done = f32[1536,768]{0,1:T(8,128)} async-done(((f32[1536,768]{0,1:T(8,128)}), f32[1536,768]{0,1:T(8,128)}) %all-reduce.17.cloned.1.call-update) | async-done | bytes 4718608 | tf_op jit(solution)/shard_map/psum | solution.py:286
  1166.5 21.2 %scatter_custom_fusion = f32[30528,192]{1,0:T(8,128)} fusion(s32[1536]{0:T(1024)} %copy-done.49, f32[1536,192]{1,0:T(8,128)S(1)} %copy.157, f32[]{:T(128)} %constant.228.clone.1), kind=kCustom, calls=%fused_computation.51 | custom fusion | flops 294912 | bytes 23446016 | tf_op jit(solution)/shard_map/scatter-add | solution.py:291
  1202.1 15.4 fusion.50
  1225.0 151.4 %reduce-scatter.11.cloned.1.call-done = f32[3816,192]{1,0:T(8,128)} async-done(((f32[30528,192]{1,0:T(8,128)}), f32[3816,192]{1,0:T(8,128)}) %reduce-scatter.11.cloned.1.call-update) | async-done | bytes 2930704 | tf_op jit(solution)/shard_map/reduce_scatter | solution.py:295
  1381.4 12.6 copy.160
  1394.1 28.0 %reduce-scatter.17.cloned.1.call-done = f32[768,96]{0,1:T(8,128)} async-done(((f32[768,768]{0,1:T(8,128)}), f32[768,96]{0,1:T(8,128)}) %reduce-scatter.17.cloned.1.call-update) | async-done | bytes 294928 | tf_op jit(solution)/shard_map/reduce_scatter | solution.py:299
  1423.7 36.1 %reduce-scatter.21.cloned.1.call-done = f32[96,2]{1,0:T(8,128)} async-done(((f32[768,2]{1,0:T(8,128)}), f32[96,2]{1,0:T(8,128)}) %reduce-scatter.21.cloned.1.call-update) | async-done | bytes 784
  1462.0 36.2 %reduce-scatter.19.cloned.1.call-done = f32[96,192]{1,0:T(8,128)} async-done(((f32[768,192]{1,0:T(8,128)}), f32[96,192]{1,0:T(8,128)}) %reduce-scatter.19.cloned.1.call-update) | async-done | bytes 73744
  1499.8 56.8 %reduce-scatter.15.cloned.1.call-done = f32[96,2,768]{2,0,1:T(8,128)} async-done(((f32[768,2,768]{2,0,1:T(8,128)}), f32[96,2,768]{2,0,1:T(8,128)}) %reduce-scatter.15.cloned.1.call-update) | async-done | bytes 589840 | tf_op jit(solution)/shard_map/reduce_scatter | solution.py:298
  1558.4 44.5 %reduce-scatter.13.cloned.1.call-done = f32[96,3,192]{2,0,1:T(8,128)} async-done(((f32[768,3,192]{2,0,1:T(8,128)}), f32[96,3,192]{2,0,1:T(8,128)}) %reduce-scatter.13.cloned.1.call-update) | async-done | bytes 221200 | tf_op jit(solution)/shard_map/reduce_scatter | solution.py:296
  1611.5 13.3 copy.158
  1624.9 53.5 %psum.39 = f32[]{:T(128)} all-reduce(f32[]{:T(128)S(6)} %add.324), channel_id=1, replica_groups=mesh['batch'=8,'mp'=4] {'batch','mp'}, use_global_device_ids=true, to_apply=%region_46.47 | all-reduce | flops 1 | bytes 8 | tf_op jit(solution)/shard_map/psum | solution.py:306
  1687.9 123.3 %all-gather.13.cloned.1.call-done = f32[3816,768]{0,1:T(8,128)} async-done(((f32[3816,192]{0,1:T(8,128)}), f32[3816,768]{0,1:T(8,128)}) %all-gather.13.cloned.1.call-update) | async-done | bytes 11722768 | tf_op jit(solution)/shard_map/all_gather | solution.py:305
  1811.3 17.3 fusion.46
  1828.6 12.3 copy.169
  1840.9 22.2 %fusion.45 = f32[3816,768]{0,1:T(8,128)} fusion(f32[3816,768]{0,1:T(8,128)} %copy.141, f32[3816,768]{0,1:T(8,128)} %get-tuple-element.440, f32[3816,768]{0,1:T(8,128)} %copy.158, f32[3816,768]{0,1:T(8,128)} %copy.160), kind=kLoop, calls=%fused_computation.57 | loop fusion | flops 41029632 | bytes 58613760 | tf_op jit(solution)/shard_map/sub | solution.py:150
  1863.2 12.3 copy.167
  1875.5 12.4 copy.171
  (331 shorter events, 224.2 us)
Async XLA Ops:
  7.2 15.7 copy-start
  7.2 87.3 %all-gather.17.cloned.1.call-start = ((), (), s32[]{:S(2)}) async-start(), calls=%async_computation.18 | async-start | bytes 13271040 | tf_op jit(solution)/shard_map/all_gather | solution.py:184
  7.3 15.6 copy-start.52
  22.8 152.7 %all-gather.15.cloned.1.call-start = ((), (), s32[]{:S(2)}) async-start(), calls=%async_computation.17 | async-start | bytes 2949120 | tf_op jit(solution)/shard_map/all_gather | solution.py:198
  31.4 81.2 %copy-start.49 = (s32[1536]{0:T(1024)}, s32[1536]{0:T(1024)S(1)}, u32[]{:S(2)}) copy-start(s32[1536]{0:T(1024)S(1)} %fusion.104) | copy-start | bytes 18436
  112.5 12.4 copy-start.12
  112.5 13.2 copy-start.30
  112.5 13.9 copy-start.25
  123.7 18.1 copy-start.35
  124.8 103.5 %all-gather.9.cloned.1.call-start = ((), (), s32[]{:S(2)}) async-start(), calls=%async_computation.7 | async-start | bytes 2654208 | tf_op jit(solution)/shard_map/all_gather | solution.py:187
  125.7 263.7 %all-reduce.11.cloned.1.call-start = ((), (), s32[]{:S(2)}) async-start(), calls=%async_computation.6 | async-start | bytes 9437184 | tf_op jit(solution)/shard_map/psum | solution.py:213
  150.7 64.7 %copy-start.10 = (bf16[192,768]{0,1:T(8,128)(2,1)}, bf16[192,768]{0,1:T(8,128)(2,1)S(1)}, u32[]{:S(2)}) copy-start(bf16[192,768]{0,1:T(8,128)(2,1)S(1)} %all_gather.30) | copy-start | bytes 884740
  151.5 27.8 %copy-start.19 = (f32[1536,32]{0,1:T(8,128)}, f32[1536,32]{0,1:T(8,128)S(1)}, u32[]{:S(2)}) copy-start(f32[1536,32]{0,1:T(8,128)S(1)} %get-tuple-element.486) | copy-start | bytes 589828
  151.5 27.8 %copy-start.21 = (f32[1536,32]{0,1:T(8,128)}, f32[1536,32]{0,1:T(8,128)S(1)}, u32[]{:S(2)}) copy-start(f32[1536,32]{0,1:T(8,128)S(1)} %get-tuple-element.487) | copy-start | bytes 589828
  218.5 196.3 %all-gather.11.cloned.1.call-start = ((), (), s32[]{:S(2)}) async-start(), calls=%async_computation.8 | async-start | bytes 1327104 | tf_op jit(solution)/shard_map/all_gather | solution.py:188
  219.2 373.9 %all-reduce.13.cloned.1.call-start = ((), (), s32[]{:S(2)}) async-start(), calls=%async_computation.9 | async-start | bytes 9437184 | tf_op jit(solution)/shard_map/psum | solution.py:221
  228.3 585.9 %copy-start.45 = (f32[768]{0:T(1024)}, f32[768]{0:T(1024)S(1)}, u32[]{:S(2)}) copy-start(f32[768]{0:T(1024)S(1)} %get-tuple-element.396) | copy-start | bytes 9220
  393.4 420.9 %copy-start.41 = (f32[1536]{0:T(1024)}, f32[1536]{0:T(1024)S(1)}, u32[]{:S(2)}) copy-start(f32[1536]{0:T(1024)S(1)} %broadcast_multiply_fusion.3) | copy-start | bytes 18436
  393.9 420.3 %copy-start.43 = (f32[1536]{0:T(1024)}, f32[1536]{0:T(1024)S(1)}, u32[]{:S(2)}) copy-start(f32[1536]{0:T(1024)S(1)} %fusion.101) | copy-start | bytes 18436
  421.0 382.6 %all-reduce.15.cloned.1.call-start = ((), (), s32[]{:S(2)}) async-start(), calls=%async_computation.10 | async-start | bytes 9437184 | tf_op jit(solution)/shard_map/psum | solution.py:261
  617.7 185.9 %copy-start.47 = (f32[1536]{0:T(1024)}, f32[1536]{0:T(1024)S(1)}, u32[]{:S(2)}) copy-start(f32[1536]{0:T(1024)S(1)} %negate_multiply_fusion.1) | copy-start | bytes 18436
  633.4 530.9 %all-reduce.17.cloned.1.call-start = ((), (), s32[]{:S(2)}) async-start(), calls=%async_computation.11 | async-start | bytes 9437184 | tf_op jit(solution)/shard_map/psum | solution.py:286
  821.5 164.0 %copy-start.20 = (f32[1536,32]{0,1:T(8,128)S(1)}, f32[1536,32]{0,1:T(8,128)}, u32[]{:S(2)}) copy-start(f32[1536,32]{0,1:T(8,128)} %copy-done.19) | copy-start | bytes 589828
  993.1 383.2 %reduce-scatter.11.cloned.1.call-start = ((), (), s32[]{:S(2)}) async-start(), calls=%async_computation.12 | async-start | bytes 35168256 | tf_op jit(solution)/shard_map/reduce_scatter | solution.py:295
  1187.7 7.5 copy-start.51
  1187.7 9.0 copy-start.9
  1187.7 234.3 %reduce-scatter.17.cloned.1.call-start = ((), (), s32[]{:S(2)}) async-start(), calls=%async_computation.15 | async-start | bytes 2654208 | tf_op jit(solution)/shard_map/reduce_scatter | solution.py:299
  1195.2 264.7 %reduce-scatter.21.cloned.1.call-start = ((), (), s32[]{:S(2)}) async-start(), calls=%async_computation.20 | async-start | bytes 442368
  1196.3 301.9 %reduce-scatter.19.cloned.1.call-start = ((), (), s32[]{:S(2)}) async-start(), calls=%async_computation.19 | async-start | bytes 884736
  1202.0 354.6 %reduce-scatter.15.cloned.1.call-start = ((), (), s32[]{:S(2)}) async-start(), calls=%async_computation.14 | async-start | bytes 5308416 | tf_op jit(solution)/shard_map/reduce_scatter | solution.py:298
  1217.5 385.3 %reduce-scatter.13.cloned.1.call-start = ((), (), s32[]{:S(2)}) async-start(), calls=%async_computation.13 | async-start | bytes 2654208 | tf_op jit(solution)/shard_map/reduce_scatter | solution.py:296
  1224.9 586.4 %all-gather.13.cloned.1.call-start = ((), (), s32[]{:S(2)}) async-start(), calls=%async_computation.16 | async-start | bytes 14745600 | tf_op jit(solution)/shard_map/all_gather | solution.py:305
  1611.5 67.6 %copy-start.13 = (f32[96,2,768]{2,1,0:T(2,128)S(1)}, f32[96,2,768]{2,1,0:T(2,128)}, u32[]{:S(2)}) copy-start(f32[96,2,768]{2,1,0:T(2,128)} %param.37) | copy-start | bytes 1769476
  1611.5 67.6 %copy-start.14 = (f32[96,2,768]{2,0,1:T(8,128)S(1)}, f32[96,2,768]{2,0,1:T(8,128)}, u32[]{:S(2)}) copy-start(f32[96,2,768]{2,0,1:T(8,128)} %reduce-scatter.15.cloned.1.call-done) | copy-start | bytes 1769476
  1611.5 67.6 %copy-start.31 = (f32[96,2,768]{2,1,0:T(2,128)S(1)}, f32[96,2,768]{2,1,0:T(2,128)}, u32[]{:S(2)}) copy-start(f32[96,2,768]{2,1,0:T(2,128)} %param.43) | copy-start | bytes 1769476
  1611.5 67.6 %copy-start.32 = (f32[96,2,768]{2,1,0:T(2,128)S(1)}, f32[96,2,768]{2,1,0:T(2,128)}, u32[]{:S(2)}) copy-start(f32[96,2,768]{2,1,0:T(2,128)} %param.49) | copy-start | bytes 1769476
  1624.8 58.6 %copy-start.54 = (f32[2,96]{1,0:T(2,128)S(1)}, f32[2,96]{1,0:T(2,128)}, u32[]{:S(2)}) copy-start(f32[2,96]{1,0:T(2,128)} %param.39) | copy-start | bytes 2308
  1624.8 58.6 %copy-start.55 = (f32[2,96]{1,0:T(2,128)S(1)}, f32[2,96]{1,0:T(2,128)}, u32[]{:S(2)}) copy-start(f32[2,96]{1,0:T(2,128)} %param.45) | copy-start | bytes 2308
  1624.8 58.6 %copy-start.56 = (f32[2,96]{1,0:T(2,128)S(1)}, f32[2,96]{1,0:T(2,128)}, u32[]{:S(2)}) copy-start(f32[2,96]{1,0:T(2,128)} %param.51) | copy-start | bytes 2308
  1624.8 59.2 %copy-start.36 = (f32[192,96]{1,0:T(8,128)S(1)}, f32[192,96]{1,0:T(8,128)}, u32[]{:S(2)}) copy-start(f32[192,96]{1,0:T(8,128)} %param.36) | copy-start | bytes 221188
  1624.8 60.9 %copy-start.24 = (f32[768,96]{0,1:T(8,128)S(1)}, f32[768,96]{0,1:T(8,128)}, u32[]{:S(2)}) copy-start(f32[768,96]{0,1:T(8,128)} %param.38) | copy-start | bytes 884740
  1624.8 60.9 %copy-start.27 = (f32[768,96]{0,1:T(8,128)S(1)}, f32[768,96]{0,1:T(8,128)}, u32[]{:S(2)}) copy-start(f32[768,96]{0,1:T(8,128)} %reduce-scatter.17.cloned.1.call-done) | copy-start | bytes 884740
  1624.8 60.9 %copy-start.37 = (f32[768,96]{0,1:T(8,128)S(1)}, f32[768,96]{0,1:T(8,128)}, u32[]{:S(2)}) copy-start(f32[768,96]{0,1:T(8,128)} %param.44) | copy-start | bytes 884740
  1679.1 7.7 copy-start.26
  1679.1 7.7 copy-start.28
  1679.1 7.7 copy-start.39
  1679.2 7.7 copy-start.40
  1875.5 12.4 copy-start.1
  (37 other events, 151.5 us)
Sparse Core Ops, SparseCore 0:
  22.9 71.4 all-gather.16
  125.0 50.4 all-gather.14
  178.0 27.8 all-gather.8
  218.6 170.7 all-reduce.10
  391.7 23.0 all-gather.10
  421.1 171.9 all-reduce.12
  633.5 170.0 all-reduce.14
  993.3 170.9 all-reduce.16
  1187.8 188.4 reduce-scatter.10
  1379.6 42.4 reduce-scatter.16
  1426.0 33.8 reduce-scatter.20
  1463.2 34.9 reduce-scatter.18
  1502.6 53.9 reduce-scatter.14
  1560.3 42.4 reduce-scatter.12
  1604.9 206.3 all-gather.12
where the time goes:
time: 1900 us
  waiting for transfers between devices  1240 us (65%)
  local copies, waits for them, and re-layouts  191 us (10%)
  matrix products  178 us (9%)
  other arithmetic  153 us (8%)
  blocking collectives  94.1 us (5%)
  between operations  21.6 us (1%)
    psum x1, waiting for transfers between devices, local(): lax.psum(jnp.dot(active_low, w_down, preferred_element_type=jnp.float32),...  171 us
    psum x1, waiting for transfers between devices, local(): lax.psum(contract(grad_qkv_low, w_qkv.reshape(D, -1), 1, 1), 'mp')  171 us
    psum x1, waiting for transfers between devices, local(): grad_one = grad_second + lax.psum(back_term, 'mp')  170 us
    psum x1, waiting for transfers between devices, local(): attn = lax.psum(attn_term, 'mp')  157 us
    reduce_scatter x1, waiting for transfers between devices, local(): lax.psum_scatter(grad_table, 'batch', scatter_dimension=0, tiled=True)  151 us
    all_gather x1, waiting for transfers between devices, local(): table_full = lax.all_gather(reduced[0], 'mp', axis=1, tiled=True)  123 us
    unnamed x132, local copies, waits for them, and re-layouts  102 us
    unnamed x17, waiting for transfers between devices  72.6 us
  transfers between devices with their start and end apart: 15, of which 14 were waited for; matrix products, arithmetic and copies ran while one was open for 8% of the time, Pallas kernels for 0%

commit v1 on v0

v1 whole, which is shorter than its diff:
```python
from functools import partial

import jax
import jax.numpy as jnp
from jax import lax
from jax.experimental import pallas as pl
from jax.experimental.pallas import tpu as pltpu
from jax.sharding import Mesh, PartitionSpec as P

HEAD_DIM = 64
SEGS = 8

peak_affinity = lax.Precision.HIGHEST
sharpness_divisor = 0.05
clip_limit = 1.0
step_number = 3.0
rates = (0.3, 0.02, 0.02, 0.02, 0.02, 0.3)
negative = -1e30
GROUP = ("x", "c")
ALL = ("h", "x", "c", "z")
f32 = jnp.float32
bf16 = jnp.bfloat16


def angles_of(places, head_dim):
    half_dim = head_dim // 2
    freqs = jnp.power(1000.0, -2.0 * jnp.arange(half_dim, dtype=f32) / head_dim)
    angles = places[:, None] * freqs[None, :]
    return jnp.cos(angles)[:, None, :], jnp.sin(angles)[:, None, :]


def rotate(values, cosine, sine):
    half_dim = values.shape[-1] // 2
    former = values[..., :half_dim]
    latter = values[..., half_dim:]
    return jnp.concatenate([former * cosine - latter * sine, latter * cosine + former * sine], -1)


def layer_norm(values, gain):
    centred = values - jnp.mean(values, -1, keepdims=True)
    spread = jnp.mean(centred * centred, -1, keepdims=True)
    return centred * lax.rsqrt(spread + 1e-05) * gain


def swiglu(gate, up):
    return jax.nn.silu(gate) * up


def dot(left, right, left_dims, right_dims, precision=None):
    return lax.dot_general(
        left, right, ((left_dims, right_dims), ((), ())), preferred_element_type=f32, precision=precision
    )


def attend_kernel(q_ref, k_ref, v_ref, segq_ref, segk_ref, o_ref):
    same = segq_ref[...] == segk_ref[...]
    query, keys, values = q_ref[...], k_ref[...], v_ref[...]
    width = query.shape[1]
    lane = lax.broadcasted_iota(jnp.int32, query.shape, 1) // HEAD_DIM
    result = jnp.zeros(query.shape, f32)
    for head in range(width // HEAD_DIM):
        own = jnp.where(lane == head, query, jnp.zeros_like(query))
        scores = dot(own, keys, (1,), (1,)) * HEAD_DIM ** (-0.5)
        scores = jnp.where(same, scores, negative)
        weights = jnp.exp(scores - jnp.max(scores, 1, keepdims=True))
        probs = (weights * (1.0 / jnp.sum(weights, 1, keepdims=True))).astype(bf16)
        result = jnp.where(lane == head, dot(probs, values, (1,), (0,)), result)
    o_ref[...] = result.astype(bf16)


def attend_back_kernel(q_ref, g_ref, k_ref, v_ref, segq_ref, segk_ref, dq_ref, dk_ref, dv_ref):
    @pl.when(pl.program_id(0) == 0)
    def _():
        dk_ref[...] = jnp.zeros_like(dk_ref)
        dv_ref[...] = jnp.zeros_like(dv_ref)

    same = segk_ref[...] == segq_ref[...]
    query, grad, keys, values = q_ref[...], g_ref[...], k_ref[...], v_ref[...]
    width = query.shape[1]
    factor = HEAD_DIM ** (-0.5)
    lane = lax.broadcasted_iota(jnp.int32, query.shape, 1) // HEAD_DIM
    result = jnp.zeros(query.shape, f32)
    for head in range(width // HEAD_DIM):
        own = jnp.where(lane == head, query, jnp.zeros_like(query))
        own_grad = jnp.where(lane == head, grad, jnp.zeros_like(grad))
        scores = dot(keys, own, (1,), (1,)) * factor
        scores = jnp.where(same, scores, negative)
        weights = jnp.exp(scores - jnp.max(scores, 0, keepdims=True))
        probs = weights * (1.0 / jnp.sum(weights, 0, keepdims=True))
        grad_probs = dot(values, own_grad, (1,), (1,))
        inner = jnp.sum(probs * grad_probs, 0, keepdims=True)
        grad_scores = (probs * (grad_probs - inner)).astype(bf16)
        dk_ref[...] += dot(grad_scores, own, (1,), (0,)) * factor
        dv_ref[...] += dot(probs.astype(bf16), own_grad, (1,), (0,))
        result = jnp.where(lane == head, dot(grad_scores, keys, (0,), (0,)) * factor, result)
    dq_ref[...] = result


def attend(query, keys, values, segment_row):
    length, width = query.shape
    block = min(256, length)
    whole = pl.BlockSpec((length, width), lambda i: (0, 0))
    part = pl.BlockSpec((block, width), lambda i: (i, 0))
    return pl.pallas_call(
        attend_kernel,
        grid=(length // block,),
        in_specs=[
            part,
            whole,
            whole,
            pl.BlockSpec((block, 1), lambda i: (i, 0)),
            pl.BlockSpec((1, length), lambda i: (0, 0)),
        ],
        out_specs=part,
        out_shape=jax.ShapeDtypeStruct((length, width), bf16),
    )(query, keys, values, segment_row[:, None], segment_row[None, :])


def attend_back(query, grad, keys, values, segment_row):
    length, width = query.shape
    block = min(256, length)
    whole = pl.BlockSpec((length, width), lambda i: (0, 0))
    part = pl.BlockSpec((block, width), lambda i: (i, 0))
    full = jax.ShapeDtypeStruct((length, width), f32)
    return pl.pallas_call(
        attend_back_kernel,
        grid=(length // block,),
        in_specs=[
            part,
            part,
            whole,
            whole,
            pl.BlockSpec((1, block), lambda i: (0, i)),
            pl.BlockSpec((length, 1), lambda i: (0, 0)),
        ],
        out_specs=[part, whole, whole],
        out_shape=[full, full, full],
    )(query, grad, keys, values, segment_row[None, :], segment_row[:, None])


MESH = pl.DeviceIdType.MESH
anywhere = pl.BlockSpec(memory_space=pl.ANY)
on_chip = pl.BlockSpec(memory_space=pltpu.VMEM)


def guarded(when, action):
    if when is None:
        action()
    else:
        pl.when(when)(action)


def both(first, second):
    return second if first is None else first if second is None else first & second


class Wires:
    def __init__(self, send_sem):
        self.at = {name: lax.axis_index(name) for name in ALL}
        self.send_sem = send_sem
        self.pending = []

    def peer(self, **moved):
        return tuple(moved.get(name, self.at[name]) for name in ALL)

    def greet(self, peers):
        barrier = pltpu.get_barrier_semaphore()
        expected = 0
        for when, target in peers:
            guarded(
                when,
                lambda target=target: pl.semaphore_signal(
                    barrier, inc=1, device_id=target, device_id_type=MESH
                ),
            )
            expected = expected + (1 if when is None else when.astype(jnp.int32))
        pl.semaphore_wait(barrier, expected)

    def send(self, source, goal, recv_sem, target, when=None):
        number = len(self.pending)

        def copy():
            return pltpu.make_async_remote_copy(
                src_ref=source,
                dst_ref=goal,
                send_sem=self.send_sem.at[number],
                recv_sem=recv_sem,
                device_id=target,
                device_id_type=MESH,
            )

        guarded(when, lambda: copy().start())
        self.pending.append((when, lambda: copy().wait_send()))

    def arrived(self, goal, recv_sem, when=None):
        guarded(when, lambda: pltpu.make_async_copy(goal, goal, recv_sem).wait())

    def drain(self):
        for when, wait in self.pending:
            guarded(when, wait)


def call(kernel, arguments, outs, out_specs, scratch, number, in_specs=None, vmem=None):
    return pl.pallas_call(
        kernel,
        in_specs=in_specs or [on_chip] * len(arguments),
        out_specs=out_specs,
        out_shape=outs,
        scratch_shapes=scratch,
        compiler_params=pltpu.CompilerParams(
            collective_id=number, has_side_effects=True, vmem_limit_bytes=vmem
        ),
    )(*arguments)


def everyone_kernel(dims, x_ref, o_ref, send_sem, recv_sem):
    wires = Wires(send_sem)
    H, X, C, Z = dims
    total = H * X * C * Z
    at = wires.at
    me = ((at["h"] * X + at["x"]) * C + at["c"]) * Z + at["z"]

    def coordinates(flat):
        return (flat // (X * C * Z), flat // (C * Z) % X, flat // Z % C, flat % Z)

    wires.greet([(None, coordinates((me + k) % total)) for k in range(1, total)])
    for k in range(1, total):
        wires.send(x_ref, o_ref.at[me], recv_sem.at[k], coordinates((me + k) % total))
    o_ref[me] = x_ref[...]
    for k in range(1, total):
        wires.arrived(o_ref.at[(me + total - k) % total], recv_sem.at[k])
    wires.drain()


def gather_everyone(x, dims, number):
    total = dims[0] * dims[1] * dims[2] * dims[3]
    if dims[0] > 2:
        return lax.all_gather(x, ALL, axis=0, tiled=False)
    return call(
        partial(everyone_kernel, dims),
        (x,),
        jax.ShapeDtypeStruct((total,) + x.shape, x.dtype),
        on_chip,
        [pltpu.SemaphoreType.DMA((total,)), pltpu.SemaphoreType.DMA((total,))],
        number,
    )


def team_kernel(dims, split_in, x_ref, o_ref, send_sem, recv_sem):
    H, X, C, Z = dims
    wires = Wires(send_sem)
    at = wires.at
    me = at["x"] * C + at["c"]
    others = [(1 - at["x"], at["c"]), (1 - at["x"], 1 - at["c"]), (at["x"], 1 - at["c"])]
    wires.greet([(None, wires.peer(x=x, c=c)) for x, c in others])
    for x, c in others:
        wires.send(x_ref.at[x * C + c], o_ref.at[me], recv_sem.at[me], wires.peer(x=x, c=c))
    o_ref[me] = x_ref[me]
    for x, c in others:
        wires.arrived(o_ref.at[x * C + c], recv_sem.at[x * C + c])
    wires.drain()


def team_swap(x, dims, number):
    if dims[0] > 2:
        return lax.all_to_all(x, GROUP, split_axis=0, concat_axis=0, tiled=True)
    return call(
        partial(team_kernel, dims, 0),
        (x,),
        jax.ShapeDtypeStruct(x.shape, x.dtype),
        on_chip,
        [pltpu.SemaphoreType.DMA((3,)), pltpu.SemaphoreType.DMA((4,))],
        number,
    )


def contrast(total, counts, queries):
    exact = partial(dot, precision=peak_affinity)
    pooled = total / counts
    scale = lax.rsqrt(jnp.sum(pooled * pooled, -1, keepdims=True) + 1e-06)
    embed = pooled * scale
    half = total.shape[0] // 2
    question, passage = embed[:half], embed[half:]
    scores = exact(question, passage, (1,), (1,)) / sharpness_divisor
    order = lax.broadcasted_iota(jnp.int32, scores.shape, 0)
    target = (order == lax.broadcasted_iota(jnp.int32, scores.shape, 1)).astype(f32)
    weight = (order < queries).astype(f32) / jnp.full(scores.shape, queries).astype(f32)
    peak = jnp.max(scores, -1, keepdims=True)
    shares = jnp.exp(scores - peak)
    mass = jnp.sum(shares, -1, keepdims=True)
    each = peak + jnp.log(mass) - jnp.sum(scores * target, -1, keepdims=True)
    loss = jnp.sum(weight[:, :1] * each)
    slope = (shares / mass - target) * weight
    grad = jnp.concatenate(
        [exact(slope, passage, (1,), (0,)), exact(slope, question, (0,), (0,))], 0
    ) / sharpness_divisor
    grad = scale * (grad - embed * jnp.sum(grad * embed, -1, keepdims=True))
    return loss, grad / counts


def contrast_kernel(dims, queries_ref, hidden_ref, seg_ref, counts_ref, loss_ref, grad_ref, sums_ref, team_ref, all_ref, send_sem, team_sem, recv_sem):
    H, X, C, Z = dims
    wires = Wires(send_sem)
    at = wires.at
    me = at["x"] * C + at["c"]
    row = at["h"] * Z + at["z"]
    rows = H * Z
    others = [(1 - at["x"], at["c"]), (1 - at["x"], 1 - at["c"]), (at["x"], 1 - at["c"])]
    far = [(row + k) % rows for k in range(1, rows)]
    wires.greet(
        [(None, wires.peer(x=x, c=c)) for x, c in others]
        + [(None, wires.peer(h=r // Z, z=r % Z)) for r in far]
    )
    texts, own_len = sums_ref.shape[0], seg_ref.shape[1]
    label = lax.broadcasted_iota(jnp.int32, (texts, own_len), 0)
    member = (label == seg_ref[...]).astype(f32)
    sums_ref[...] = dot(member, hidden_ref[...], (1,), (0,), peak_affinity)
    for x, c in others:
        wires.send(sums_ref, team_ref.at[me], team_sem.at[me], wires.peer(x=x, c=c))
    team_ref[me] = sums_ref[...]
    for x, c in others:
        wires.arrived(team_ref.at[x * C + c], team_sem.at[x * C + c])
    all_ref[row] = (team_ref[0] + team_ref[1]) + (team_ref[2] + team_ref[3])
    for r in far:
        wires.send(all_ref.at[row], all_ref.at[row], recv_sem.at[row], wires.peer(h=r // Z, z=r % Z))
    for r in far:
        wires.arrived(all_ref.at[r], recv_sem.at[r])
    wires.drain()
    width = all_ref.shape[2]
    loss, grad = contrast(all_ref[...].reshape(rows * texts, width), counts_ref[...], queries_ref[0])
    loss_ref[...] = jnp.full(loss_ref.shape, loss)
    all_ref[...] = grad.reshape(rows, texts, width)
    grad_ref[...] = dot(member, all_ref[row], (0,), (0,), peak_affinity)


def contrast_all(hidden, seg_own, counts, queries, dims, number):
    H, X, C, Z = dims
    rows, team = H * Z, X * C
    own_len, width = hidden.shape
    labels = jnp.arange(SEGS, dtype=jnp.int32)
    if H > 2:
        member = (seg_own[None, :] == labels[:, None]).astype(f32)
        sums = jnp.dot(member, hidden, precision=peak_affinity)
        total = lax.all_gather(lax.psum(sums, GROUP), ("h", "z"), axis=0, tiled=True)
        loss, grad = contrast(total, counts, queries[0])
        row = lax.axis_index("h") * Z + lax.axis_index("z")
        grad = lax.dynamic_slice_in_dim(grad, row * SEGS, SEGS, 0)
        return loss, dot(member, grad, (0,), (0,), peak_affinity)
    loss, grad = call(
        partial(contrast_kernel, dims),
        (queries, hidden, seg_own[None, :], counts),
        [jax.ShapeDtypeStruct((8, 128), f32), jax.ShapeDtypeStruct(hidden.shape, f32)],
        [on_chip] * 2,
        [
            pltpu.VMEM((SEGS, width), f32),
            pltpu.VMEM((team, SEGS, width), f32),
            pltpu.VMEM((rows, SEGS, width), f32),
            pltpu.SemaphoreType.DMA((3 + rows,)),
            pltpu.SemaphoreType.DMA((team,)),
            pltpu.SemaphoreType.DMA((rows,)),
        ],
        number,
        in_specs=[pl.BlockSpec(memory_space=pltpu.SMEM)] + [on_chip] * 3,
        vmem=12 * 2**20,
    )
    return loss[0, 0], grad


def fetch_kernel(dims, x_ref, o_ref, send_sem, recv_sem):
    H, X, C, Z = dims
    wires = Wires(send_sem)
    at = wires.at
    h, x, c = at["h"], at["x"], at["c"]
    across, beside = wires.peer(x=1 - x), wires.peer(c=1 - c)
    away = [(h + k) % H for k in range(1, H)]
    wires.greet([(None, across), (None, beside)] + [(None, wires.peer(h=g)) for g in away])
    for g in away:
        wires.send(x_ref.at[g], o_ref.at[x, c, h], recv_sem.at[x, c, h], wires.peer(h=g))
    mine = (o_ref.at[x, c, h], recv_sem.at[x, c, h])
    wires.send(x_ref.at[h], *mine, across)
    wires.send(x_ref.at[h], *mine, beside)
    o_ref[x, c, h] = x_ref[h]
    for g in away:
        place = (o_ref.at[x, c, g], recv_sem.at[x, c, g])
        wires.arrived(*place)
        wires.send(place[0], *place, across)
        wires.send(place[0], *place, beside)
    for g in [h] + away:
        place = (o_ref.at[1 - x, c, g], recv_sem.at[1 - x, c, g])
        wires.arrived(*place)
        wires.send(place[0], *place, beside)
    for y in (x, 1 - x):
        for g in [h] + away:
            wires.arrived(o_ref.at[y, 1 - c, g], recv_sem.at[y, 1 - c, g])
    wires.drain()


def fetch_rows(rows, dims, number):
    H, X, C, Z = dims
    if H > 2:
        got = lax.all_to_all(rows, "h", split_axis=0, concat_axis=0, tiled=True)
        return lax.all_gather(got, GROUP, axis=0, tiled=False)
    return call(
        partial(fetch_kernel, dims),
        (rows,),
        jax.ShapeDtypeStruct((X, C) + rows.shape, rows.dtype),
        on_chip,
        [pltpu.SemaphoreType.DMA((4 * H,)), pltpu.SemaphoreType.DMA((X, C, H))],
        number,
    )


def along_line(wires, piece, recv_sem, extra=None):
    z, Z = wires.at["z"], wires.size_z
    right, left = wires.peer(z=z + 1), wires.peer(z=z - 1)
    for far in range(0, Z):
        for sign, onward, more in ((-1, right, z + 1 < Z), (1, left, z >= 1)):
            spot = z + sign * far
            there = None if far == 0 else (spot >= 0 if sign < 0 else spot < Z)
            for view, sem in zip(piece(spot), recv_sem(spot)):
                if far:
                    wires.arrived(view, sem, there)
                wires.send(view, view, sem, onward, both(there, more))
            if extra is not None and (far or sign < 0):
                extra(spot, there)


def settle_kernel(dims, x_ref, o_ref, beside_ref, across_ref, ready_ref, send_sem, beside_sem, across_sem, recv_sem):
    H, X, C, Z = dims
    wires = Wires(send_sem)
    wires.size_z = Z
    at = wires.at
    h, x, c, z = at["h"], at["x"], at["c"], at["z"]
    across, beside = wires.peer(x=1 - x), wires.peer(c=1 - c)
    away = [(h + k) % H for k in range(1, H)]
    wires.greet(
        [(None, across), (None, beside)]
        + [(None, wires.peer(h=g)) for g in away]
        + [(z + 1 < Z, wires.peer(z=z + 1)), (z >= 1, wires.peer(z=z - 1))]
    )
    for y in (1 - x, x):
        wires.send(x_ref.at[y, 1 - c], beside_ref.at[y], beside_sem.at[y], beside)
    wires.arrived(beside_ref.at[1 - x], beside_sem.at[1 - x])
    for g in away + [h]:
        total = x_ref[1 - x, c, g].astype(f32) + beside_ref[1 - x, g].astype(f32)
        ready_ref[g] = total.astype(ready_ref.dtype)
        wires.send(ready_ref.at[g], across_ref.at[g], across_sem.at[g], across)
    wires.arrived(beside_ref.at[x], beside_sem.at[x])
    for g in away + [h]:
        wires.arrived(across_ref.at[g], across_sem.at[g])
        total = x_ref[x, c, g].astype(f32) + beside_ref[x, g].astype(f32)
        total = (total + across_ref[g].astype(f32)).astype(o_ref.dtype)
        if g is h:
            o_ref[z, h] = total
        else:
            ready_ref[H + g] = total
            wires.send(ready_ref.at[H + g], o_ref.at[z, h], recv_sem.at[z, h], wires.peer(h=g))
    for g in away:
        wires.arrived(o_ref.at[z, g], recv_sem.at[z, g])
    along_line(wires, lambda s: [o_ref.at[s]], lambda s: [recv_sem.at[s, H]])
    wires.drain()


def settle_rows(terms, dims, number):
    H, X, C, Z = dims
    block = terms.shape[3:]
    if H > 2:
        terms = terms.reshape((X * C,) + (H,) + block)
        terms = lax.psum_scatter(terms, GROUP, scatter_dimension=0, tiled=True)[0]
        terms = lax.all_to_all(terms, "h", split_axis=0, concat_axis=0, tiled=True)
        return lax.all_gather(terms, "z", axis=0, tiled=False)
    return call(
        partial(settle_kernel, dims),
        (terms,),
        jax.ShapeDtypeStruct((Z, H) + block, terms.dtype),
        on_chip,
        [
            pltpu.VMEM((X, H) + block, terms.dtype),
            pltpu.VMEM((H,) + block, terms.dtype),
            pltpu.VMEM((2 * H,) + block, terms.dtype),
            pltpu.SemaphoreType.DMA((2 + 2 * H + 2 * Z,)),
            pltpu.SemaphoreType.DMA((X,)),
            pltpu.SemaphoreType.DMA((H,)),
            pltpu.SemaphoreType.DMA((Z, H + 1)),
        ],
        number,
    )


def gather_weights(pieces, dims):
    H, X, C, Z = dims
    rows = pieces[0].shape[0]
    outs = [lax.all_gather(piece, ALL, axis=0, tiled=False) for piece in pieces]
    outs = [whole.reshape(H * X * C, Z, rows, -1).transpose(1, 0, 2, 3) for whole in outs]
    return [whole.reshape(Z, H * X * C * rows, -1) for whole in outs]


def reduce_weights(pieces, dims):
    H, X, C, Z = dims
    batch = H * X * C
    rows = pieces[0].shape[1] // batch
    sums = []
    for piece in pieces:
        piece = piece.reshape(Z, batch, rows, -1).transpose(1, 0, 2, 3)
        piece = piece.reshape(batch * Z, rows, -1)
        sums.append(lax.psum_scatter(piece, ALL, scatter_dimension=0, tiled=True)[0].astype(f32))
    return sums


class Spread:
    def __init__(self, wires, dims, kinds, stages, outs, send_sem, recv_sem):
        self.wires, self.kinds, self.stages, self.outs = wires, kinds, stages, outs
        self.send_sem, self.recv_sem = send_sem, recv_sem
        self.Z = dims[3]
        self.spots = 2 * self.Z - 1

    def where(self, i):
        z = self.wires.at["z"]
        if isinstance(i, int) and i == 0:
            return z, 0, None
        sign = 1 - 2 * (i % 2)
        s = z + sign * ((i + 1) // 2)
        return s, sign, (s >= 0) & (s < self.Z)

    def place(self, a, s, h, x, c):
        return self.outs[a].at[s, h, x, c], self.recv_sem.at[a, s, (h * 2 + x) * 2 + c]

    def moves(self, phase, i):
        at, peer = self.wires.at, self.wires.peer
        h, x, c, z = at["h"], at["x"], at["c"], at["z"]
        s, sign, there = self.where(i)
        beside = peer(c=1 - c)
        moves = []

        def add(a, block, kind, target, when=there):
            view, sem = self.place(a, s, *block)
            fresh = isinstance(i, int) and i == 0 and phase < 2
            source = self.stages[a] if fresh else view
            moves.append((when, source, view, sem, self.send_sem.at[a, kind, i], target))

        for a, kind in enumerate(self.kinds):
            hops = [peer(h=1 - h), peer(x=1 - x)]
            if phase == 0:
                if isinstance(i, int) and i == 0:
                    add(a, (h, x, c), 0, peer(z=z + 1), z + 1 < self.Z)
                    add(a, (h, x, c), 1, peer(z=z - 1), z >= 1)
                else:
                    onward = z - sign
                    add(a, (h, x, c), 0, peer(z=onward), there & (onward >= 0) & (onward < self.Z))
            if phase == 1:
                add(a, (h, x, c), 2, hops[kind])
                add(a, (h, x, c), 3, hops[1 - kind])
                add(a, (h, x, c), 4, beside)
            if phase == 2:
                block = (1 - h, x, c) if kind == 0 else (h, 1 - x, c)
                add(a, block, 5, hops[1 - kind])
                add(a, block, 6, beside)
            if phase == 3:
                add(a, (h, 1 - x, c) if kind == 0 else (1 - h, x, c), 7, beside)
                add(a, (1 - h, 1 - x, c), 8, beside)
        return moves

    def copy(self, move):
        return pltpu.make_async_remote_copy(
            src_ref=move[1],
            dst_ref=move[2],
            send_sem=move[4],
            recv_sem=move[3],
            device_id=move[5],
            device_id_type=MESH,
        )

    def wait(self, phase, i):
        at = self.wires.at
        h, x, c = at["h"], at["x"], at["c"]
        s, _, there = self.where(i)
        for a, kind in enumerate(self.kinds):
            if phase == 0:
                blocks = [] if isinstance(i, int) and i == 0 else [(h, x, c)]
            elif phase == 1:
                blocks = []
            elif phase == 2:
                blocks = [(1 - h, x, c) if kind == 0 else (h, 1 - x, c)]
            elif phase == 3:
                blocks = [(h, 1 - x, c) if kind == 0 else (1 - h, x, c), (1 - h, 1 - x, c)]
            else:
                blocks = [(g, y, 1 - c) for g in range(2) for y in range(2)]
            for block in blocks:
                self.wires.arrived(*self.place(a, s, *block), there)

    def step(self, phase, i):
        self.wait(phase, i)
        if phase < 4:
            for move in self.moves(phase, i):
                guarded(move[0], lambda move=move: self.copy(move).start())

    def run(self, phases, first, last):
        if first == 0:
            for phase in phases:
                self.step(phase, 0)
        low = max(first, 1)
        if low < last:

            @pl.loop(low, last)
            def _(i):
                for phase in phases:
                    self.step(phase, i)

    def settle(self):
        def sent(i):
            for phase in (0, 1, 2, 3):
                for move in self.moves(phase, i):
                    guarded(move[0], lambda move=move: self.copy(move).wait_send())

        sent(0)

        @pl.loop(1, self.spots)
        def _(i):
            sent(i)


class Late:
    def __init__(self, wires, dims, stage, out, send_sem, recv_sem):
        self.wires, self.stage, self.out = wires, stage, out
        self.send_sem, self.recv_sem, self.Z = send_sem, recv_sem, dims[3]
        self.spots = 2 * self.Z - 1

    def where(self, i):
        z = self.wires.at["z"]
        if isinstance(i, int) and i == 0:
            return z, 0, None
        sign = 1 - 2 * (i % 2)
        s = z + sign * ((i + 1) // 2)
        return s, sign, (s >= 0) & (s < self.Z)

    def line(self, s, c):
        return self.out.at[s, :, :, c]

    def moves(self, i):
        at, peer = self.wires.at, self.wires.peer
        h, x, c, z = at["h"], at["x"], at["c"], at["z"]
        sent, got = self.send_sem, self.recv_sem
        if isinstance(i, str) and i == "across":
            view = self.out.at[z, h, x, c]
            return [(None, self.stage, view, sent.at[0, 0], got.at[0, 0], peer(x=1 - x))]
        if isinstance(i, str) and i == "away":
            view = self.out.at[z, h, :, c]
            return [(None, view, view, sent.at[0, 1], got.at[0, 1], peer(h=1 - h))]
        s, sign, there = self.where(i)
        view = self.line(s, c)
        if isinstance(i, int) and i == 0:
            moves = [
                (z + 1 < self.Z, view, view, sent.at[1, 0], got.at[1, s], peer(z=z + 1)),
                (z >= 1, view, view, sent.at[0, 2], got.at[1, s], peer(z=z - 1)),
            ]
        else:
            onward = z - sign
            when = there & (onward >= 0) & (onward < self.Z)
            moves = [(when, view, view, sent.at[1, i], got.at[1, s], peer(z=onward))]
        return moves + [(there, view, view, sent.at[2, i], got.at[2, s], peer(c=1 - c))]

    def copy(self, move):
        return pltpu.make_async_remote_copy(
            src_ref=move[1],
            dst_ref=move[2],
            send_sem=move[3],
            recv_sem=move[4],
            device_id=move[5],
            device_id_type=MESH,
        )

    def step(self, i):
        at = self.wires.at
        h, x, c, z = at["h"], at["x"], at["c"], at["z"]
        if isinstance(i, str) and i == "away":
            self.wires.arrived(self.out.at[z, h, 1 - x, c], self.recv_sem.at[0, 0])
        elif isinstance(i, int) and i == 0:
            self.wires.arrived(self.out.at[z, 1 - h, :, c], self.recv_sem.at[0, 1])
        elif not isinstance(i, str):
            s, _, there = self.where(i)
            self.wires.arrived(self.line(s, c), self.recv_sem.at[1, s], there)
        for move in self.moves(i):
            guarded(move[0], lambda move=move: self.copy(move).start())

    def settle(self):
        def sent(i):
            for move in self.moves(i):
                guarded(move[0], lambda move=move: self.copy(move).wait_send())

        for i in ("across", "away", 0):
            sent(i)

        @pl.loop(1, self.spots)
        def _(i):
            sent(i)

        @pl.loop(0, self.Z)
        def _(s):
            self.wires.arrived(self.line(s, 1 - self.wires.at["c"]), self.recv_sem.at[2, s])


def selection(rows, columns, shift):
    row = lax.broadcasted_iota(jnp.int32, (rows, columns), 0)
    column = lax.broadcasted_iota(jnp.int32, (rows, columns), 1)
    return (column == row + shift).astype(bf16)


def turned(values, cosine, sine):
    half = HEAD_DIM // 2
    lanes = values.shape[1]
    lane = lax.broadcasted_iota(jnp.int32, values.shape, 1) % HEAD_DIM
    after = pltpu.roll(values, lanes - half, 1)
    before = pltpu.roll(values, half, 1)
    wide = lambda t: jnp.concatenate([t] * (lanes // t.shape[1]), 1)
    return values * wide(cosine) + jnp.where(lane < half, -after, before) * wide(sine)


def attend_block(query, keys, values, same, heads):
    lane = lax.broadcasted_iota(jnp.int32, query.shape, 1) // HEAD_DIM
    result = jnp.zeros(query.shape, f32)
    for head in range(heads):
        own = jnp.where(lane == head, query, jnp.zeros_like(query))
        scores = dot(own, keys, (1,), (1,)) * HEAD_DIM ** (-0.5)
        scores = jnp.where(same, scores, negative)
        weights = jnp.exp(scores - jnp.max(scores, 1, keepdims=True))
        probs = (weights * (1.0 / jnp.sum(weights, 1, keepdims=True))).astype(bf16)
        result = jnp.where(lane == head, dot(probs, values, (1,), (0,)), result)
    return result.astype(bf16)


def front_kernel(
    dims,
    rows_ref,
    slot_ref,
    more_ref,
    cos_ref,
    sin_ref,
    segq_ref,
    segk_ref,
    *refs,
):
    ins, outs, (x_ref, q_ref, k_ref, v_ref, swap_ref), stages = refs[:5], refs[5:10], refs[10:15], refs[15:20]
    (
        got_ref,
        heads_ref,
        pick_ref,
        send_ref,
        load_sem,
        store_sem,
        main_send,
        main_recv,
        small_send,
        small_recv,
        late_send,
        late_recv,
        row_send,
        row_recv,
        heads_sem,
        swap_send,
        swap_recv,
    ) = refs[20:]
    H, X, C, Z = dims
    wires = Wires(row_send)
    at = wires.at
    h, x, c, z = at["h"], at["x"], at["c"], at["z"]
    across, beside, away = wires.peer(x=1 - x), wires.peer(c=1 - c), wires.peer(h=1 - h)
    team = x * C + c
    wires.greet(
        [(None, across), (None, beside), (None, away), (None, wires.peer(x=1 - x, c=1 - c))]
        + [(z + 1 < Z, wires.peer(z=z + 1)), (z >= 1, wires.peer(z=z - 1))]
    )
    loads = [pltpu.make_async_copy(ins[i], stages[i], load_sem.at[i]) for i in range(5)]
    stores = [
        pltpu.make_async_copy(stages[i], outs[i].at[z, h, x, c], store_sem.at[i]) for i in range(5)
    ]
    for load in loads:
        load.start()

    def owner_rows(y, d, g):
        return got_ref.at[y, d, g], row_recv.at[y, d, g]

    wires.send(rows_ref.at[1 - h], *owner_rows(x, c, h), away)
    wires.send(rows_ref.at[h], *owner_rows(x, c, h), across)
    wires.send(rows_ref.at[h], *owner_rows(x, c, h), beside)
    got_ref[x, c, h] = rows_ref[h]
    for load, store in zip(loads, stores):
        load.wait()
        store.start()
    small = Spread(wires, dims, [1], stages[:1], outs[:1], small_send, small_recv)
    main = Spread(wires, dims, [0, 0, 1], stages[1:4], outs[1:4], main_send, main_recv)
    late = Late(wires, dims, stages[4], outs[4], late_send, late_recv)
    spots = main.spots
    small.run((0, 1), 0, 1)
    late.step("across")
    main.run((0,), 0, 1)
    small.run((0, 1), 1, 3)
    place = owner_rows(x, c, 1 - h)
    wires.arrived(*place)
    wires.send(place[0], *place, across)
    wires.send(place[0], *place, beside)
    small.run((2,), 0, 1)
    main.run((0,), 1, 3)
    stores[4].wait()
    late.step("away")
    small.run((0, 1), 3, 5)
    small.run((2,), 1, 3)
    for g in (h, 1 - h):
        place = owner_rows(1 - x, c, g)
        wires.arrived(*place)
        wires.send(place[0], *place, beside)
    small.run((3,), 0, 1)
    small.run((0, 1), 5, spots)
    main.run((0,), 3, 5)
    small.run((2,), 3, 5)
    small.run((3,), 1, 3)
    late.step(0)
    small.run((2,), 5, spots)
    main.run((1,), 0, 3)
    main.run((0,), 5, spots)
    main.run((1,), 3, spots)
    small.run((3,), 3, spots)
    stores[0].wait()
    small.run((4,), 0, spots)
    heads = pltpu.make_async_copy(outs[0].at[team], heads_ref, heads_sem)
    heads.start()
    for y in (x, 1 - x):
        for g in (h, 1 - h):
            wires.arrived(*owner_rows(y, 1 - c, g))
    heads.wait()

    length, width = x_ref.shape
    heads_width = send_ref.shape[1]
    lanes = q_ref.shape[1]
    merged = heads_ref[...].reshape(width, heads_ref.shape[-1])
    for part in range(3):
        choose = selection(lanes, 3 * heads_width, part * heads_width)
        row = lax.broadcasted_iota(jnp.int32, choose.shape, 0)
        choose = jnp.where(row < heads_width, choose, jnp.zeros_like(choose))
        pick_ref[part] = dot(merged, choose, (1,), (1,)).astype(bf16)
    block = min(256, length)
    blocks = length // block
    slots = got_ref.shape[0] * got_ref.shape[1] * got_ref.shape[2] * got_ref.shape[3]

    @pl.loop(0, blocks)
    def _(i):
        here = pl.ds(pl.multiple_of(i * block, block), block)
        slot = lax.broadcasted_iota(jnp.int32, (block, slots), 1)
        chosen = (slot_ref[here, :] == slot).astype(bf16)
        full = dot(chosen, got_ref[...].reshape(slots, width), (1,), (0,))
        low = (full + more_ref[here, :].astype(f32)).astype(bf16)
        x_ref[here, :] = low
        cosine, sine = cos_ref[here, :], sin_ref[here, :]
        q_ref[here, :] = turned(dot(low, pick_ref[0], (1,), (0,)), cosine, sine).astype(bf16)
        k_ref[here, :] = turned(dot(low, pick_ref[1], (1,), (0,)), cosine, sine).astype(bf16)
        v_ref[here, :] = dot(low, pick_ref[2], (1,), (0,)).astype(bf16)

        @pl.when(i == 2)
        def _():
            late.step(1)
            late.step(2)

    main.run((2,), 0, 3)
    own_len = length // (X * C)

    @pl.loop(0, blocks)
    def _(i):
        here = pl.ds(pl.multiple_of(i * block, block), block)
        same = segq_ref[here, :] == segk_ref[...]
        heads = heads_width // HEAD_DIM
        result = attend_block(q_ref[here, :], k_ref[...], v_ref[...], same, heads)
        send_ref[here, :] = result[:, :heads_width]

        @pl.when((i == 0) | (i == 2))
        def _():
            main.step(2, i + 3)
            main.step(2, i + 4)

        @pl.when(i == 1)
        def _():
            late.step(3)
            late.step(4)

        pl.when(i == 3)(lambda: main.step(3, 0))
        pl.when(i == 4)(lambda: main.step(3, 1))

    others = [(1 - x, c), (1 - x, 1 - c), (x, 1 - c)]

    def part_of(y, d):
        return send_ref.at[pl.ds(pl.multiple_of((y * C + d) * own_len, 128), own_len), :]

    swaps = [
        pltpu.make_async_remote_copy(
            src_ref=part_of(y, d),
            dst_ref=swap_ref.at[team],
            send_sem=swap_send.at[k],
            recv_sem=swap_recv.at[team],
            device_id=wires.peer(x=y, c=d),
            device_id_type=MESH,
        )
        for k, (y, d) in enumerate(others)
    ]
    for swap in swaps:
        swap.start()
    swap_ref[team] = send_ref[pl.ds(pl.multiple_of(team * own_len, 128), own_len), :]
    late.step(5)
    late.step(6)
    main.run((3,), 2, spots)
    main.run((4,), 0, spots)
    for y, d in others:
        wires.arrived(swap_ref.at[y * C + d], swap_recv.at[y * C + d])
    for swap in swaps:
        swap.wait_send()
    for store in stores[1:4]:
        store.wait()
    late.settle()
    main.settle()
    small.settle()
    wires.drain()


def front(rows, slot, more, cosine, sine, segments, pieces, heads_width, dims, number):
    H, X, C, Z = dims
    length, width = more.shape
    team = X * C
    spots = 2 * Z - 1
    batch = H * team
    rows_in = pieces[0].shape[0]
    lanes = -(-heads_width // 128) * 128
    vmem = lambda shape, dtype=bf16: pltpu.VMEM(shape, dtype)
    dma = lambda *shape: pltpu.SemaphoreType.DMA(shape)
    outs = call(
        partial(front_kernel, dims),
        (rows, slot[:, None], more, cosine, sine, segments[:, None], segments[None, :], *pieces),
        [jax.ShapeDtypeStruct((Z, H, X, C) + piece.shape, bf16) for piece in pieces]
        + [jax.ShapeDtypeStruct((length, width), bf16)]
        + [jax.ShapeDtypeStruct((length, lanes), bf16)] * 3
        + [jax.ShapeDtypeStruct((team, length // team, heads_width), bf16)],
        [anywhere] * 5 + [on_chip] * 5,
        [vmem(piece.shape) for piece in pieces]
        + [
            vmem((X, C) + rows.shape),
            vmem((H, X, C) + pieces[0].shape),
            vmem((3, width, lanes)),
            vmem((length, heads_width)),
            dma(5),
            dma(5),
            dma(3, 9, spots),
            dma(3, Z, batch),
            dma(1, 9, spots),
            dma(1, Z, batch),
            dma(3, spots),
            dma(3, Z),
            dma(7),
            dma(X, C, H),
            pltpu.SemaphoreType.DMA,
            dma(3),
            dma(team),
        ],
        number,
        in_specs=[on_chip] * 7 + [anywhere] * 5,
        vmem=60 * 2**20,
    )
    weights = [whole.reshape(Z, batch * rows_in, -1) for whole in outs[:5]]
    return weights, outs[5:]


def sum_rows(goal, sources):
    rows = goal.shape[0]
    step = 16 if rows % 16 == 0 else rows

    @pl.loop(0, rows // step)
    def _(i):
        part = pl.ds(pl.multiple_of(i * step, step), step)
        value = sources[0][part, :].astype(f32)
        for source in sources[1:]:
            value += source[part, :].astype(f32)
        goal[part, :] = value.astype(goal.dtype)


class Line:
    def __init__(self, wires, Z, buffers, send_sem, recv_sem):
        self.wires, self.Z, self.buffers = wires, Z, buffers
        self.send_sem, self.recv_sem = send_sem, recv_sem

    def onward(self, a, s, source):
        z = self.wires.at["z"]
        upward = z < s
        goal = jnp.where(upward, z + 1, z - 1)
        index = jnp.where((s < goal) | upward, s, self.Z)
        return pltpu.make_async_remote_copy(
            src_ref=source,
            dst_ref=self.buffers[a].at[index],
            send_sem=self.send_sem.at[a, s],
            recv_sem=self.recv_sem.at[a, index],
            device_id=self.wires.peer(z=goal),
            device_id_type=MESH,
        )

    def step(self, a, s, sources, running, final):
        z, Z = self.wires.at["z"], self.Z

        def took(index):
            view = self.buffers[a].at[index]
            self.wires.arrived(view, self.recv_sem.at[a, index])
            return view

        passing = z != s
        edge = ((z < s) & (z == 0)) | ((z > s) & (z == Z - 1))

        @pl.when(passing & edge)
        def _():
            sum_rows(running, sources)

        @pl.when(passing & ~edge)
        def _():
            sum_rows(running, sources + [took(s)])

        @pl.when(passing)
        def _():
            self.onward(a, s, running).start()

        @pl.when((z == s) & (z == 0))
        def _():
            sum_rows(final, sources + [took(Z)])

        @pl.when((z == s) & (z == Z - 1))
        def _():
            sum_rows(final, sources + [took(s)])

        @pl.when((z == s) & (z > 0) & (z < Z - 1))
        def _():
            sum_rows(final, sources + [took(s), took(Z)])

    def settle(self, a, s, running):
        @pl.when(self.wires.at["z"] != s)
        def _():
            self.onward(a, s, running).wait_send()


class Gathering:
    def __init__(self, wires, dims, kinds, ins, outs, own, near, first, second, lines, sems):
        self.wires, self.kinds, self.Z = wires, kinds, dims[3]
        self.ins, self.outs, self.own, self.near = ins, outs, own, near
        self.first, self.second = first, second
        self.load_sem, self.near_sem, self.first_sem, self.second_sem = sems[:4]
        self.near_send, self.first_send, self.second_send = sems[4:7]
        self.line = Line(wires, dims[3], lines, sems[7], sems[8])
        at = wires.at
        self.x, self.h, self.c, self.z = at["x"], at["h"], at["c"], at["z"]
        self.across, self.beside = wires.peer(x=1 - self.x), wires.peer(c=1 - self.c)
        self.away = wires.peer(h=1 - self.h)

    def turn(self, i):
        Z = self.Z
        low = self.z < Z // 2
        side = jnp.where(low, self.z, Z - 1 - self.z)
        s = jnp.where(i < Z - 1 - side, Z - 1 - i, jnp.where(i < Z - 1, i - (Z - 1 - side), side))
        return jnp.where(low, s, Z - 1 - s)

    def remote(self, source, goal, send_sem, recv_sem, target):
        return pltpu.make_async_remote_copy(
            src_ref=source,
            dst_ref=goal,
            send_sem=send_sem,
            recv_sem=recv_sem,
            device_id=target,
            device_id_type=MESH,
        )

    def load(self, a, s):
        return pltpu.make_async_copy(
            self.ins[a].at[s, :, :, self.c], self.own[a].at[s], self.load_sem.at[a, s]
        )

    def near_copy(self, a, s):
        return self.remote(
            self.ins[a].at[s, :, :, 1 - self.c],
            self.near[a].at[s],
            self.near_send.at[a, s],
            self.near_sem.at[a, s],
            self.beside,
        )

    def axes(self, a):
        return (self.x, self.h) if self.kinds[a] == 0 else (self.h, self.x)

    def spot(self, a, s, f, g):
        return (s, g, f) if self.kinds[a] == 0 else (s, f, g)

    def first_copy(self, a, s, g):
        f, _ = self.axes(a)
        return self.remote(
            self.own[a].at[self.spot(a, s, 1 - f, g)],
            self.first[a].at[s, g],
            self.first_send.at[a, s, g],
            self.first_sem.at[a, s, g],
            self.across if self.kinds[a] == 0 else self.away,
        )

    def second_copy(self, a, s):
        f, g = self.axes(a)
        return self.remote(
            self.own[a].at[self.spot(a, s, f, 1 - g)],
            self.second[a].at[s],
            self.second_send.at[a, s],
            self.second_sem.at[a, s],
            self.away if self.kinds[a] == 0 else self.across,
        )

    def begin(self):
        @pl.loop(0, self.Z)
        def _(i):
            s = self.turn(i)
            for a in range(len(self.kinds)):
                self.near_copy(a, s).start()
                self.load(a, s).start()

    def one(self, i):
        s = self.turn(i)
        for a in range(len(self.kinds)):
            self.wires.arrived(self.near[a].at[s], self.near_sem.at[a, s])
            self.load(a, s).wait()
            f, g = self.axes(a)
            for k in (1 - g, g):
                place = self.spot(a, s, 1 - f, k)
                sum_rows(self.own[a].at[place], [self.own[a].at[place], self.near[a].at[place]])
                self.first_copy(a, s, k).start()

    def two(self, i):
        s = self.turn(i)
        for a in range(len(self.kinds)):
            f, g = self.axes(a)
            for k in (1 - g, g):
                self.wires.arrived(self.first[a].at[s, k], self.first_sem.at[a, s, k])
            place = self.spot(a, s, f, 1 - g)
            sum_rows(
                self.own[a].at[place],
                [self.own[a].at[place], self.near[a].at[place], self.first[a].at[s, 1 - g]],
            )
            self.second_copy(a, s).start()

    def three(self, i):
        s = self.turn(i)
        for a in range(len(self.kinds)):
            f, g = self.axes(a)
            self.wires.arrived(self.second[a].at[s], self.second_sem.at[a, s])
            place = self.spot(a, s, f, g)
            own = self.own[a].at[place]
            sources = [own, self.near[a].at[place], self.first[a].at[s, g], self.second[a].at[s]]
            self.line.step(a, s, sources, own, self.outs[a])

    def settle(self):
        @pl.loop(0, self.Z)
        def _(s):
            for a in range(len(self.kinds)):
                self.near_copy(a, s).wait_send()
                for k in range(2):
                    self.first_copy(a, s, k).wait_send()
                self.second_copy(a, s).wait_send()
                f, g = self.axes(a)
                self.line.settle(a, s, self.own[a].at[self.spot(a, s, f, g)])


def attend_back_block(query, grad, keys, values, same, heads, dk_ref, dv_ref):
    factor = HEAD_DIM ** (-0.5)
    lane = lax.broadcasted_iota(jnp.int32, query.shape, 1) // HEAD_DIM
    result = jnp.zeros(query.shape, f32)
    for head in range(heads):
        own = jnp.where(lane == head, query, jnp.zeros_like(query))
        own_grad = jnp.where(lane == head, grad, jnp.zeros_like(grad))
        scores = dot(keys, own, (1,), (1,)) * factor
        scores = jnp.where(same, scores, negative)
        weights = jnp.exp(scores - jnp.max(scores, 0, keepdims=True))
        probs = weights * (1.0 / jnp.sum(weights, 0, keepdims=True))
        grad_probs = dot(values, own_grad, (1,), (1,))
        inner = jnp.sum(probs * grad_probs, 0, keepdims=True)
        grad_scores = (probs * (grad_probs - inner)).astype(bf16)
        dk_ref[...] += dot(grad_scores, own, (1,), (0,)) * factor
        dv_ref[...] += dot(probs.astype(bf16), own_grad, (1,), (0,))
        result = jnp.where(lane == head, dot(grad_scores, keys, (0,), (0,)) * factor, result)
    return result


def back_kernel(
    dims,
    heads,
    swap_ref,
    q_ref,
    k_ref,
    v_ref,
    x_ref,
    cos_ref,
    sin_ref,
    segq_ref,
    segk_ref,
    slot_ref,
    first_ref,
    listq_ref,
    listk_ref,
    heads_ref,
    in_gate,
    in_up,
    in_down,
    in_misc,
    out_gate,
    out_up,
    out_down,
    out_misc,
    out_qkv,
    spread_ref,
    zero_ref,
    total_ref,
    *scratch,
):
    H, X, C, Z = dims
    scratch = list(scratch)
    take = lambda n: [scratch.pop(0) for _ in range(n)]
    own, near, first, second, lines = (take(4) for _ in range(5))
    (got_ref, grad_ref, dk_ref, dv_ref, low_ref, matrix_ref, heads_v) = take(7)
    (qsrc, qnear, qx, qh, qtot, qline) = take(6)
    (slots_ref, beside_ref, across_ref, ready_ref) = take(4)
    sems = take(9)
    (swap_send, swap_recv, heads_sem, qsend, qrecv, qline_send, qline_recv) = take(7)
    (row_send, beside_sem, across_sem, row_recv, norm_ref, norm_send, norm_recv) = take(7)
    wires = Wires(row_send)
    wires.size_z = Z
    at = wires.at
    h, x, c, z = at["h"], at["x"], at["c"], at["z"]
    across, beside, away = wires.peer(x=1 - x), wires.peer(c=1 - c), wires.peer(h=1 - h)
    team = x * C + c
    devices = H * X * C * Z
    me = (team + h * X * C) * Z + z

    def coordinates(flat):
        return (flat // (X * C * Z), flat // (C * Z) % X, flat // Z % C, flat % Z)

    wires.greet([(None, coordinates((me + k) % devices)) for k in range(1, devices)])
    others = [(1 - x, c), (1 - x, 1 - c), (x, 1 - c)]
    swaps = [
        pltpu.make_async_remote_copy(
            src_ref=swap_ref.at[y * C + d],
            dst_ref=got_ref.at[team],
            send_sem=swap_send.at[k],
            recv_sem=swap_recv.at[team],
            device_id=wires.peer(x=y, c=d),
            device_id_type=MESH,
        )
        for k, (y, d) in enumerate(others)
    ]
    for swap in swaps:
        swap.start()
    fetch = pltpu.make_async_copy(heads_ref.at[team], heads_v, heads_sem)
    fetch.start()
    job = Gathering(
        wires,
        dims,
        [1, 1, 0, 0],
        [in_gate, in_up, in_down, in_misc],
        [out_gate, out_up, out_down, out_misc],
        own,
        near,
        first,
        second,
        lines,
        sems,
    )
    job.begin()
    got_ref[team] = swap_ref[team]
    dk_ref[...] = jnp.zeros_like(dk_ref)
    dv_ref[...] = jnp.zeros_like(dv_ref)
    matrix_ref[...] = jnp.zeros_like(matrix_ref)
    length, lanes = q_ref.shape
    heads_width = got_ref.shape[2]
    own_len = got_ref.shape[1]
    width = x_ref.shape[1]
    edge = (z == 0) | (z == Z - 1)
    job.one(0)
    widen = selection(heads_width, lanes, 0)
    for y, d in others:
        wires.arrived(got_ref.at[y * C + d], swap_recv.at[y * C + d])
    job.one(1)

    @pl.loop(0, X * C)
    def _(k):
        part = pl.ds(pl.multiple_of(k * own_len, 128), own_len)
        grad_ref[part, :] = dot(got_ref[k], widen, (1,), (0,)).astype(bf16)

    block = min(256, length)
    blocks = length // block

    def narrow(values, part):
        choose = selection(lanes, 3 * heads_width, part * heads_width)
        row = lax.broadcasted_iota(jnp.int32, choose.shape, 0)
        choose = jnp.where(row < heads_width, choose, jnp.zeros_like(choose))
        return dot(values.astype(bf16), choose, (1,), (0,))

    @pl.loop(0, blocks)
    def _(i):
        here = pl.ds(pl.multiple_of(i * block, block), block)
        same = segk_ref[...] == segq_ref[:, here]
        grad_query = attend_back_block(
            q_ref[here, :], grad_ref[here, :], k_ref[...], v_ref[...], same, heads, dk_ref, dv_ref
        )
        low_ref[here, :] = narrow(turned(grad_query, cos_ref[here, :], -sin_ref[here, :]), 0).astype(bf16)

        pl.when((i == 1) | (i == 3))(lambda: job.two(i // 2))
        pl.when((i == 2) | (i == 5))(lambda: job.one(2 + i // 5))
        pl.when((i == 4) & edge)(lambda: job.three(0))

    fetch.wait()

    @pl.loop(0, X * C)
    def _(k):
        part = pl.ds(pl.multiple_of(k * own_len, 128), own_len)
        grad_keys = turned(dk_ref[part, :], cos_ref[part, :], -sin_ref[part, :])
        low = low_ref[part, :].astype(f32) + narrow(grad_keys, 1) + narrow(dv_ref[part, :], 2)
        low = low.astype(bf16)
        zero = dot(low, heads_v[...], (1,), (1,))
        zero_ref[part, :] = (zero + (k == team).astype(f32) * first_ref[...]).astype(bf16)
        matrix_ref[...] += dot(x_ref[part, :], low, (0,), (0,))
        pl.when(k == 1)(lambda: job.two(2))
        pl.when(k == 2)(lambda: job.three(edge.astype(jnp.int32)))

    capacity = slots_ref.shape[3]

    def fill(y, d):
        for g in range(H):
            slot = lax.broadcasted_iota(jnp.int32, (capacity, length), 0)
            slot += ((y * C + d) * H + g) * capacity
            chosen = (slot_ref[...] == slot).astype(bf16)
            slots_ref[y, d, g] = dot(chosen, zero_ref[...], (1,), (0,)).astype(bf16)

    def row_copy(y):
        wires.send(slots_ref.at[y, 1 - c], beside_ref.at[y], beside_sem.at[y], beside)

    fill(1 - x, 1 - c)
    row_copy(1 - x)
    fill(x, 1 - c)
    row_copy(x)
    fill(1 - x, c)
    wires.arrived(beside_ref.at[1 - x], beside_sem.at[1 - x])
    for g in (1 - h, h):
        total = slots_ref[1 - x, c, g].astype(f32) + beside_ref[1 - x, g].astype(f32)
        ready_ref[g] = total.astype(bf16)
        wires.send(ready_ref.at[g], across_ref.at[g], across_sem.at[g], across)
    fill(x, c)
    rows_in, wide = qsrc.shape[3], qsrc.shape[4]
    qsrc[...] = matrix_ref[...].astype(bf16).reshape(qsrc.shape)

    def qcopy(source, goal, k, target):
        return pltpu.make_async_remote_copy(
            src_ref=source,
            dst_ref=goal,
            send_sem=qsend.at[k],
            recv_sem=qrecv.at[k],
            device_id=target,
            device_id_type=MESH,
        )

    qcopies = [
        qcopy(qsrc.at[:, :, 1 - c], qnear, 0, beside),
        qcopy(qsrc.at[:, 1 - x, c], qx.at[0], 1, across),
        qcopy(qnear.at[:, 1 - x], qx.at[1], 2, across),
        qcopy(qsrc.at[1 - h, x, c], qh.at[0], 3, away),
        qcopy(qnear.at[1 - h, x], qh.at[1], 4, away),
        qcopy(qx.at[0, 1 - h], qh.at[2], 5, away),
        qcopy(qx.at[1, 1 - h], qh.at[3], 6, away),
    ]
    qcopies[0].start()
    wires.arrived(beside_ref.at[x], beside_sem.at[x])
    job.three(2)
    pl.when(~edge)(lambda: job.three(1))
    for g in (1 - h, h):
        wires.arrived(across_ref.at[g], across_sem.at[g])
        total = slots_ref[x, c, g].astype(f32) + beside_ref[x, g].astype(f32)
        total = (total + across_ref[g].astype(f32)).astype(bf16)
        if g is h:
            spread_ref[z, h] = total
        else:
            ready_ref[2 + g] = total
            wires.send(ready_ref.at[2 + g], spread_ref.at[z, h], row_recv.at[z, h], away)
    wires.arrived(qnear, qrecv.at[0])
    for k in range(1, 5):
        qcopies[k].start()
    job.two(3)
    wires.arrived(spread_ref.at[z, 1 - h], row_recv.at[z, 1 - h])

    def row_line(far):
        for sign in (-1, 1):
            spot = z + sign * far
            onward = z - sign
            more = (onward >= 0) & (onward < Z)
            there = None if far == 0 else (spot >= 0) & (spot < Z)
            if far:
                wires.arrived(spread_ref.at[spot], row_recv.at[spot, H], there)
            wires.send(
                spread_ref.at[spot], spread_ref.at[spot], row_recv.at[spot, H], wires.peer(z=onward), both(there, more)
            )

    row_line(0)
    for k in (1, 2):
        wires.arrived(qx.at[k - 1], qrecv.at[k])
    qcopies[5].start()
    qcopies[6].start()
    row_line(1)
    for k in range(4):
        wires.arrived(qh.at[k], qrecv.at[3 + k])
    terms = [qsrc.at[h, x, c], qnear.at[h, x], qx.at[0, h], qx.at[1, h]]
    pair = (team, x * C + 1 - c, (1 - x) * C + c, (1 - x) * C + 1 - c)
    for k in range(4):
        sum_rows(qtot.at[pair[k]], [terms[k], qh.at[k]])
    line = Line(wires, Z, [qline], qline_send, qline_recv)

    def heads_line(i):
        s = job.turn(i)
        line.step(0, s, [qtot.at[s]], qtot.at[s], out_qkv)

    pl.loop(0, 2)(heads_line)
    for far in range(2, Z - 1):
        row_line(far)
    pl.loop(2, Z - 1)(heads_line)
    row_line(Z - 1)
    heads_line(Z - 1)
    job.three(3)
    quarter = H * capacity
    mine = pl.ds(pl.multiple_of(z * quarter, 8), quarter)
    products = dot(
        spread_ref[z].reshape(quarter, width), spread_ref[...].reshape(Z * quarter, width), (1,), (1,)
    )
    squares = jnp.sum(jnp.where(listq_ref[mine, :] == listk_ref[...], products, 0.0))
    for ref in (out_gate, out_up, out_down, out_qkv):
        squares += jnp.sum(ref[...] * ref[...])
    lane = lax.broadcasted_iota(jnp.int32, out_misc.shape, 1)
    squares += jnp.sum(out_misc[...] * out_misc[...] * jnp.where(lane < heads_width, 1.0, 1.0 / Z))
    norm_ref[me] = jnp.full(norm_ref.shape[1:], squares)

    @pl.loop(0, Z)
    def _(s):
        line.settle(0, s, qtot.at[s])

    for copy in qcopies:
        copy.wait_send()
    for swap in swaps:
        swap.wait_send()
    job.settle()
    wires.drain()
    tell = [
        pltpu.make_async_remote_copy(
            src_ref=norm_ref.at[me],
            dst_ref=norm_ref.at[me],
            send_sem=norm_send.at[k],
            recv_sem=norm_recv.at[k],
            device_id=coordinates((me + k) % devices),
            device_id_type=MESH,
        )
        for k in range(1, devices)
    ]
    for copy in tell:
        copy.start()
    for k in range(1, devices):
        wires.arrived(norm_ref.at[(me + devices - k) % devices], norm_recv.at[k])
    total_ref[...] = jnp.sum(norm_ref[...], 0)
    for copy in tell:
        copy.wait_send()


def back(swap, q, k, v, x_low, cosine, sine, segments, slot, listed, grad_first, w_heads, terms, heads, capacity, dims, number):
    H, X, C, Z = dims
    length, width = x_low.shape
    lanes = q.shape[1]
    team, own_len, heads_width = swap.shape
    batch = H * team
    rows = width // batch
    widths = [term.shape[2] for term in terms]
    wide = 3 * heads_width
    vmem = lambda shape, dtype=bf16: pltpu.VMEM(shape, dtype)
    dma = lambda *shape: pltpu.SemaphoreType.DMA(shape)
    shapes = [(Z, H, X), (Z, H, X), (Z, 2), (Z,), (Z + 1,)]
    n = len(terms)
    return call(
        partial(back_kernel, dims, heads),
        (
            swap,
            q,
            k,
            v,
            x_low,
            cosine,
            sine,
            segments[None, :],
            segments[:, None],
            slot[None, :],
            grad_first,
            listed[:, None],
            listed[None, :],
            w_heads,
            *(term.reshape(Z, H, X, C, rows, -1) for term in terms),
        ),
        [jax.ShapeDtypeStruct((rows, w), f32) for w in widths + [wide]]
        + [
            jax.ShapeDtypeStruct((Z, H, capacity, width), bf16),
            jax.ShapeDtypeStruct((length, width), bf16),
            jax.ShapeDtypeStruct((8, 128), f32),
        ],
        [on_chip] * 8,
        [vmem(shape + (rows, w)) for shape in shapes for w in widths]
        + [
            vmem(swap.shape),
            vmem((length, lanes)),
            vmem((length, lanes), f32),
            vmem((length, lanes), f32),
            vmem((length, wide)),
            vmem((width, wide), f32),
            vmem(w_heads.shape[1:]),
            vmem((H, X, C, rows, wide)),
            vmem((H, X, rows, wide)),
            vmem((2, H, rows, wide)),
            vmem((4, rows, wide)),
            vmem((Z, rows, wide)),
            vmem((Z + 1, rows, wide)),
            vmem((X, C, H, capacity, width)),
            vmem((X, H, capacity, width)),
            vmem((H, capacity, width)),
            vmem((2 * H, capacity, width)),
            dma(n, Z),
            dma(n, Z),
            dma(n, Z, 2),
            dma(n, Z),
            dma(n, Z),
            dma(n, Z, 2),
            dma(n, Z),
            dma(n, Z),
            dma(n, Z + 1),
            dma(3),
            dma(team),
            pltpu.SemaphoreType.DMA,
            dma(7),
            dma(7),
            dma(1, Z),
            dma(1, Z + 1),
            dma(2 + 2 + 1 + 2 * Z),
            dma(X),
            dma(H),
            dma(Z, H + 1),
            vmem((batch * Z, 8, 128), f32),
            dma(batch * Z),
            dma(batch * Z),
        ],
        number,
        in_specs=[on_chip] * 13 + [anywhere] * 5,
        vmem=67_000_000,
    )


def adam_update(weight, grad, first, second, rate):
    first = 0.5 * first + 0.5 * grad
    second = 0.5 * second + 0.5 * grad * grad
    correction = 1.0 - 0.5**step_number
    weight = weight - rate * (
        first / correction / (jnp.sqrt(second / correction) + 1e-08) + 0.01 * weight
    )
    return (weight, first, second)


def blank(shape, dtype):
    return pl.pallas_call(
        lambda o_ref: None, out_specs=anywhere, out_shape=jax.ShapeDtypeStruct(shape, dtype)
    )()


def rows_kernel(list_ref, table_ref, o_ref, hold_ref, sem):
    count = o_ref.shape[0]

    @pl.loop(0, count)
    def _(i):
        row = pl.ds(list_ref[i], 1)
        pltpu.make_async_copy(table_ref.at[row, :], hold_ref.at[pl.ds(i, 1), :], sem).start()

    pltpu.make_async_copy(hold_ref, hold_ref, sem).wait()
    o_ref[...] = hold_ref[...].astype(bf16)


def low_rows(table, listed):
    shape = (listed.shape[0], table.shape[1])
    return pl.pallas_call(
        rows_kernel,
        in_specs=[pl.BlockSpec(memory_space=pltpu.SMEM), anywhere],
        out_specs=on_chip,
        out_shape=jax.ShapeDtypeStruct(shape, bf16),
        scratch_shapes=[pltpu.VMEM(shape, f32), pltpu.SemaphoreType.DMA],
    )(listed, table)


def table_kernel(rate, rounds_ref, scale_ref, list_ref, rows_ref, more_ref, w_ref, m_ref, v_ref, nw_ref, g_ref, nv_ref, far_ref, sem):
    block, width = w_ref.shape
    count = list_ref.shape[1]
    start = pl.program_id(0) * block

    def placed(turn, rows):
        row = lax.broadcasted_iota(jnp.int32, (block, count), 0) + start
        pick = (row == list_ref[pl.ds(turn, 1), :]).astype(bf16)
        return dot(pick, rows, (1,), (0,))

    g_ref[...] = placed(0, rows_ref[...])

    @pl.loop(1, rounds_ref[0])
    def _(turn):
        copy = pltpu.make_async_copy(more_ref.at[turn - 1], far_ref, sem)
        copy.start()
        copy.wait()
        g_ref[...] += placed(turn, far_ref[...])

    grad = g_ref[...] * scale_ref[0]
    new_w, _, new_v = adam_update(w_ref[...], grad, m_ref[...], v_ref[...], rate)
    g_ref[...] = grad
    nw_ref[...] = new_w
    nv_ref[...] = new_v


def update_table(rounds, scale, lists, rows, more, table, first, second, rate):
    height, width = table.shape
    sizes = [n for n in range(8, 513, 8) if height % n == 0]
    block = max(sizes) if sizes else height
    part = pl.BlockSpec((block, width), lambda i: (i, 0))
    whole = lambda a: pl.BlockSpec(a.shape, lambda i: (0,) * a.ndim)
    single = pl.BlockSpec(memory_space=pltpu.SMEM)
    return pl.pallas_call(
        partial(table_kernel, rate),
        grid=(height // block,),
        in_specs=[single, single, whole(lists), whole(rows), anywhere, part, part, part],
        out_specs=[part] * 3,
        out_shape=[jax.ShapeDtypeStruct(table.shape, f32)] * 3,
        scratch_shapes=[pltpu.VMEM(rows.shape, bf16), pltpu.SemaphoreType.DMA],
        compiler_params=pltpu.CompilerParams(vmem_limit_bytes=56 * 2**20),
    )(rounds.reshape(1), scale.reshape(1), lists, rows, more, table, first, second)


def small_kernel(scale_ref, qkv_ref, misc_ref, gate_ref, up_ref, down_ref, *refs):
    ins, outs = refs[:15], refs[15:]
    scale = scale_ref[0]
    heads_width = ins[0].shape[2]
    turned_misc = misc_ref[...].T

    def update(k, grad, where):
        old, first, second = (ins[3 * k + n][where] for n in range(3))
        for n, value in enumerate(adam_update(old, grad * scale, first, second, rates[1 + k])):
            outs[3 * k + n][where] = value

    for part in range(3):
        grad = qkv_ref[:, part * heads_width : (part + 1) * heads_width]
        update(0, grad, (slice(None), part, slice(None)))
    update(1, turned_misc[:heads_width], (slice(None), slice(None)))
    update(2, gate_ref[...], (slice(None), 0, slice(None)))
    update(2, up_ref[...], (slice(None), 1, slice(None)))
    update(3, down_ref[...].T, (slice(None), slice(None)))
    count = ins[12].shape[0]
    update(4, turned_misc[heads_width : heads_width + count], (slice(None), slice(None)))


def update_small(scale, sums, olds, firsts, seconds):
    values = [value for group in zip(olds, firsts, seconds) for value in group]
    whole = lambda a: pl.BlockSpec(a.shape, lambda i: (0,) * a.ndim)
    outs = pl.pallas_call(
        small_kernel,
        grid=(1,),
        in_specs=[pl.BlockSpec(memory_space=pltpu.SMEM)] + [whole(a) for a in (*sums, *values)],
        out_specs=[whole(a) for a in values],
        out_shape=[jax.ShapeDtypeStruct(value.shape, f32) for value in values],
        compiler_params=pltpu.CompilerParams(vmem_limit_bytes=50 * 2**20),
    )(scale.reshape(1), *sums, *values)
    return [tuple(outs[3 * k : 3 * k + 3]) for k in range(len(olds))]


def local(
    dims,
    token_ids,
    segment_ids,
    row_of,
    query_count,
    table,
    qkv_weight,
    out_weight,
    gate_up_weight,
    down_weight,
    gains,
    table_m,
    qkv_m,
    out_m,
    gate_up_m,
    down_m,
    gains_m,
    table_v,
    qkv_v,
    out_v,
    gate_up_v,
    down_v,
    gains_v,
):
    H, X, C, Z = dims
    G = X * C
    batch = H * G
    at = {name: lax.axis_index(name) for name in ALL}
    team = at["x"] * C + at["c"]
    owner = at["h"] * G + team
    length = token_ids.shape[1]
    own_len = length // G
    part_len = length // Z
    shard_rows, width = table.shape
    rows_in = width // batch
    heads_width = qkv_weight.shape[2]
    ff_part = down_weight.shape[0]
    capacity = -(-3 * length // (64 * batch)) * 16

    position = jnp.arange(length, dtype=jnp.int32)
    start = at["z"] * part_len
    mine = lax.dynamic_slice_in_dim(token_ids[0], start, part_len, 0)
    mine_seg = lax.dynamic_slice_in_dim(segment_ids[0], start, part_len, 0)
    earlier = position[None, :] < (start + position[:part_len])[:, None]
    seen = jnp.any((mine[:, None] == token_ids[0][None, :]) & earlier, 1)
    tags = jnp.stack([row_of[mine] * 2 + seen.astype(jnp.int32), mine_seg])
    everyone = gather_everyone(tags, dims, 0)
    tags_all = everyone[:, 0].reshape(batch, length)
    segs_all = everyone[:, 1].reshape(batch, length)
    ids_all, fresh_all = tags_all // 2, tags_all % 2 == 0
    row = at["h"] * Z + at["z"]
    seg_row = lax.dynamic_index_in_dim(segs_all, row, 0, keepdims=False)
    ids_row = lax.dynamic_index_in_dim(ids_all, row, 0, keepdims=False)
    fresh_row = lax.dynamic_index_in_dim(fresh_all, row, 0, keepdims=False)

    def counted(flags):
        lanes = 128 if length % 128 == 0 else length
        steps = flags.astype(f32).reshape(-1, length // lanes, lanes)
        upto = jnp.arange(lanes)[:, None] <= jnp.arange(lanes)[None, :]
        inner = jnp.einsum("rgl,lk->rgk", steps, upto.astype(f32))
        sums = inner[:, :, -1]
        groups = jnp.arange(length // lanes)
        before = (groups[:, None] < groups[None, :]).astype(f32)
        outer = jnp.dot(sums, before, precision=peak_affinity)
        return (inner + outer[:, :, None]).reshape(-1, length).astype(jnp.int32)

    owned = fresh_all & (ids_all // shard_rows == owner)
    number = counted(owned)
    shares = (ids_all // shard_rows)[:, None, :] == jnp.arange(batch, dtype=jnp.int32)[None, :, None]
    shares = jnp.sum((shares & fresh_all[:, None, :]).astype(jnp.int32), 2)
    rounds = (jnp.max(shares) + capacity - 1) // capacity
    offset = jnp.where(owned, number, 0)
    spot = jnp.arange(1, capacity + 1, dtype=jnp.int32)

    def owned_list(turn, rows):
        ids = lax.dynamic_slice_in_dim(ids_all, rows[0], rows[1], 0) if rows else ids_all
        places = lax.dynamic_slice_in_dim(offset, rows[0], rows[1], 0) if rows else offset
        hit = (spot + turn * capacity)[None, :, None] == places[:, None, :]
        return jnp.sum(jnp.where(hit, (ids - owner * shard_rows + 1)[:, None, :], 0), 2) - 1

    holder_row = ids_row // shard_rows
    holders = jnp.arange(batch, dtype=jnp.int32)
    split = fresh_row[None, :] & (holder_row[None, :] == holders[:, None])
    number_row = jnp.sum(jnp.where(split, counted(split), 0), 0)
    same_row = ids_row[:, None] == ids_row[None, :]
    rank_row = jnp.sum(jnp.where(same_row, number_row[None, :], 0), 1) - 1
    slots = batch * capacity

    def listed_for(turn):
        return owned_list(turn, None).reshape(H, Z, capacity).transpose(1, 0, 2).reshape(-1)

    def slot_of(turn):
        rank = rank_row - turn * capacity
        slot = ((holder_row % G) * H + holder_row // G) * capacity + rank
        return jnp.where((rank >= 0) & (rank < capacity), slot, -1)

    def expander(turn):
        slot = slot_of(turn)
        return (slot[:, None] == jnp.arange(slots, dtype=jnp.int32)[None, :]).astype(bf16)

    labels = jnp.arange(SEGS, dtype=jnp.int32)
    marks = jnp.arange(SEGS + 1, dtype=jnp.int32)
    member_row = (seg_row[:, None] == marks[None, :]).astype(jnp.int32)
    counts_row = jnp.sum(member_row, 0)
    starts = jnp.cumsum(counts_row) - counts_row
    places = (position - jnp.sum(member_row * starts[None, :], 1)).astype(f32)
    cosine, sine = angles_of(places, HEAD_DIM)
    heads = heads_width // HEAD_DIM

    def rows_for(turn):
        listed = jnp.concatenate([owned_list(turn, (h * Z + at["z"], 1)) for h in range(H)])
        return low_rows(table, jnp.maximum(listed, 0).reshape(-1)).reshape(H, capacity, width)

    def fetch(turn):
        got = fetch_rows(rows_for(turn), dims, 1).reshape(slots, width)
        return jnp.dot(expander(turn), got, preferred_element_type=f32).astype(bf16)

    _, x_more = lax.while_loop(
        lambda s: s[0] < rounds,
        lambda s: (s[0] + 1, s[1] + fetch(s[0])),
        (jnp.int32(1), jnp.zeros((length, width), bf16)),
    )

    pad = -(-(heads_width + 2) // 128) * 128 - heads_width
    misc = jnp.concatenate([out_weight.T, gains.T, jnp.zeros((rows_in, pad - 2), f32)], 1)
    pieces = [
        qkv_weight.reshape(rows_in, -1).astype(bf16),
        misc.astype(bf16),
        gate_up_weight[:, 0].astype(bf16),
        gate_up_weight[:, 1].astype(bf16),
        down_weight.T.astype(bf16),
    ]
    if H == 2:
        tables = [jnp.concatenate([t[:, 0]] * 4, 1) for t in (cosine, sine)]
        weights, (x_low, query, keys, values, attended) = front(
            rows_for(0), slot_of(0), x_more, *tables, seg_row, pieces, heads_width, dims, 2
        )
    else:
        weights = gather_weights(pieces, dims)
    w_qkv, w_misc, w_gate, w_up, w_down = weights
    w_out = w_misc[:, :, :heads_width]
    gain = w_misc[0, :, heads_width : heads_width + 2].T.astype(f32)
    if H != 2:
        w_heads = lax.dynamic_index_in_dim(w_qkv, team, 0, keepdims=False)
        x_low = x_more + fetch(0)
        qkv = jnp.dot(x_low, w_heads, preferred_element_type=f32).reshape(length, 3, heads, HEAD_DIM)
        query = rotate(qkv[:, 0], cosine, sine).astype(bf16).reshape(length, -1)
        keys = rotate(qkv[:, 1], cosine, sine).astype(bf16).reshape(length, -1)
        values = qkv[:, 2].astype(bf16).reshape(length, -1)
        attended_heads = attend(query, keys, values, seg_row)
        attended = team_swap(attended_heads.reshape(G, own_len, heads_width), dims, 3)
    attended = attended.transpose(1, 0, 2)
    x_own = lax.dynamic_slice_in_dim(x_low, team * own_len, own_len, 0)

    attn = dot(attended, w_out, (1, 2), (0, 2))
    hidden_one, first_back = jax.vjp(layer_norm, x_own.astype(f32) + attn, gain[0])
    hidden_low = hidden_one.astype(bf16)
    gate = jnp.einsum("td,zdf->ztf", hidden_low, w_gate, preferred_element_type=f32)
    up = jnp.einsum("td,zdf->ztf", hidden_low, w_up, preferred_element_type=f32)
    active, swiglu_back = jax.vjp(swiglu, gate, up)
    active_low = active.astype(bf16)
    mlp = dot(active_low, w_down, (0, 2), (0, 2))
    hidden_two, second_back = jax.vjp(layer_norm, hidden_one + mlp, gain[1])

    seg_own = lax.dynamic_slice_in_dim(seg_row, team * own_len, own_len, 0)
    counts_all = jnp.sum((segs_all[:, None, :] == labels[None, :, None]).astype(f32), -1)
    loss_value, grad_two = contrast_all(
        hidden_two, seg_own, counts_all.reshape(-1, 1), query_count, dims, 4
    )

    grad_second, grad_gain_two = second_back(grad_two)
    grad_mlp_low = grad_second.astype(bf16)
    grad_active = jnp.einsum("tn,znf->ztf", grad_mlp_low, w_down, preferred_element_type=f32)
    grad_down = jnp.einsum("tn,ztf->znf", grad_mlp_low, active_low, preferred_element_type=f32)
    grad_gate, grad_up = swiglu_back(grad_active)
    grad_gate_low, grad_up_low = grad_gate.astype(bf16), grad_up.astype(bf16)
    grad_one = grad_second + dot(grad_gate_low, w_gate, (0, 2), (0, 2))
    grad_one = grad_one + dot(grad_up_low, w_up, (0, 2), (0, 2))
    grad_first, grad_gain_one = first_back(grad_one)
    weight_grad = partial(jnp.einsum, "td,ztf->zdf", preferred_element_type=f32)
    grad_gate = weight_grad(hidden_low, grad_gate_low).astype(bf16)
    grad_up = weight_grad(hidden_low, grad_up_low).astype(bf16)
    grad_attn_low = grad_first.astype(bf16)
    grad_attended = jnp.einsum("tn,znk->tzk", grad_attn_low, w_out, preferred_element_type=f32)
    grad_attended = grad_attended.astype(bf16).transpose(1, 0, 2)
    grad_out = jnp.einsum("tn,tzk->znk", grad_attn_low, attended, preferred_element_type=f32)
    grad_gains = jnp.stack([grad_gain_one, grad_gain_two], 1)
    grad_misc = jnp.concatenate(
        [
            grad_out.astype(bf16),
            jnp.broadcast_to(grad_gains.astype(bf16)[None], (Z, width, 2)),
            jnp.zeros((Z, width, pad - 2), bf16),
        ],
        2,
    )
    terms = [grad_gate, grad_up, grad_down.astype(bf16), grad_misc]
    most_rounds = -(-length // capacity)
    listed = listed_for(0)
    _, lists = lax.while_loop(
        lambda s: s[0] < rounds,
        lambda s: (
            s[0] + 1,
            lax.dynamic_update_slice_in_dim(s[1], listed_for(s[0])[None], s[0], 0),
        ),
        (jnp.int32(1), jnp.broadcast_to(listed[None], (most_rounds,) + listed.shape)),
    )
    if H == 2:
        sum_gate, sum_up, sum_down, sum_misc, sum_qkv, spread, grad_zero_low, total = back(
            grad_attended,
            query,
            keys,
            values,
            x_low,
            *tables,
            seg_row,
            slot_of(0),
            listed,
            grad_first,
            w_qkv,
            terms,
            heads,
            capacity,
            dims,
            5,
        )
    else:
        grad_heads = team_swap(grad_attended, dims, 5).reshape(length, heads_width)
        grad_query, grad_keys, grad_values = attend_back(query, grad_heads, keys, values, seg_row)
        back_turn = lambda g: rotate(g.reshape(length, heads, HEAD_DIM), cosine, -sine).reshape(length, -1)
        grad_qkv_low = jnp.concatenate([back_turn(grad_query), back_turn(grad_keys), grad_values], 1)
        grad_qkv_low = grad_qkv_low.astype(bf16)
        grad_heads_w = dot(x_low, grad_qkv_low, (0,), (0,)).astype(bf16)
        grad_zero = dot(grad_qkv_low, w_heads, (1,), (1,))
        own_term = lax.dynamic_update_slice_in_dim(
            jnp.zeros_like(grad_zero), grad_first, team * own_len, 0
        )
        grad_zero_low = (grad_zero + own_term).astype(bf16)
        heads_grad = lax.dynamic_update_slice_in_dim(
            jnp.zeros((Z,) + grad_heads_w.shape, bf16), grad_heads_w[None], team, 0
        )
        sum_gate, sum_up, sum_down, sum_misc, sum_qkv = reduce_weights(terms + [heads_grad], dims)

    def collect(turn):
        terms = dot(expander(turn), grad_zero_low, (0,), (0,)).astype(bf16)
        terms = terms.reshape(X, C, H, capacity, width)
        return settle_rows(terms, dims, 6)

    flat = lambda rows: rows.reshape(Z * H * capacity, width)
    spread = flat(spread if H == 2 else collect(0))

    def between(left, left_list, right, right_list):
        same = left_list[:, None] == right_list[None, :]
        return jnp.sum(jnp.where(same, dot(left, right, (1,), (1,)), 0.0))

    def summed(squares):
        return jnp.sum(gather_everyone(jnp.full((8, 128), squares), dims, 8), 0)

    def further(state):
        turn, more, total = state
        rows = flat(collect(turn))
        listed = lists[turn]
        squares = between(rows, listed, rows, listed) + 2 * between(rows, listed, spread, lists[0])
        squares += 2 * lax.fori_loop(
            1, turn, lambda k, held: held + between(rows, listed, more[k - 1], lists[k]), jnp.zeros((), f32)
        )
        more = lax.dynamic_update_slice_in_dim(more, rows[None], turn - 1, 0)
        return turn + 1, more, total + summed(squares / Z)

    if H != 2:
        squares = between(spread, listed, spread, listed) + jnp.sum(sum_misc[:, heads_width:] ** 2)
        squares = squares / Z + jnp.sum(sum_misc[:, :heads_width] ** 2)
        for part in (sum_qkv, sum_gate, sum_up, sum_down):
            squares += jnp.sum(part * part)
        total = summed(squares)
    blank_rows = blank((max(most_rounds - 1, 1),) + spread.shape, bf16)
    _, more, total = lax.while_loop(
        lambda s: s[0] < rounds, further, (jnp.int32(1), blank_rows, total)
    )
    grad_norm = jnp.sqrt(total[0, 0])
    scale = clip_limit / jnp.maximum(grad_norm, clip_limit)
    new_table, clipped_table, new_table_v = update_table(
        rounds, scale, lists, spread, more, table, table_m, table_v, rates[0]
    )
    updated = update_small(
        scale,
        (sum_qkv, sum_misc, sum_gate, sum_up, sum_down),
        (qkv_weight, out_weight, gate_up_weight, down_weight, gains),
        (qkv_m, out_m, gate_up_m, down_m, gains_m),
        (qkv_v, out_v, gate_up_v, down_v, gains_v),
    )
    return (
        loss_value.reshape(1),
        grad_norm.reshape(1),
        new_table,
        *(new[0] for new in updated),
        clipped_table,
        *(new[1] for new in updated),
        new_table_v,
        *(new[2] for new in updated),
    )


def solution(mesh):
    batch, mp = mesh.shape["batch"], mesh.shape["mp"]
    dims = (batch // mp, mp // 2, 2, mp)
    split = Mesh(mesh.devices.reshape(dims), ALL)
    rows = ("h", "x", "c")
    weights = (
        P(rows, None),
        P(rows, None, "z"),
        P("z", rows),
        P(rows, None, "z"),
        P("z", rows),
        P(None, rows),
    )
    return jax.shard_map(
        partial(local, dims),
        mesh=split,
        in_specs=(P(rows, None), P(rows, None), P(), P()) + weights * 3,
        out_specs=(P(), P()) + weights + weights + weights,
        check_vma=False,
    )
```

time: 1900 us -> 432 us (0.23)
  waiting for transfers between devices: 1240 us -> 0 us
  Pallas kernels: 0 us -> 302 us
  local copies, waits for them, and re-layouts: 191 us -> 36.2 us
  other arithmetic: 153 us -> 23.6 us
  matrix products: 178 us -> 57.1 us
  blocking collectives: 94.1 us -> 0 us
    psum x4 -> x0, waiting for transfers between devices: 669 us -> none  [the longest x1 171 us: local(): lax.psum(jnp.dot(active_low, w_down, preferred_element_type=jnp.float32),...]
    pallas_call x0 -> x8, Pallas kernels: none -> 302 us  [the longest x4 260 us: call(): pl.pallas_call(kernel, in_specs=in_specs or [on_chip] * len(arguments), o...]
    reduce_scatter x4 -> x0, waiting for transfers between devices: 281 us -> none  [the longest x1 151 us: local(): lax.psum_scatter(grad_table, 'batch', scatter_dimension=0, tiled=True)]
    all_gather x5 -> x0, waiting for transfers between devices: 218 us -> none  [the longest x1 123 us: local(): table_full = lax.all_gather(reduced[0], 'mp', axis=1, tiled=True)]
    dot_general x37 -> x15, matrix products: 173 us -> 55 us  [the longest x1 13.5 us: local(): up = jnp.einsum('td,zdf->ztf', hidden_low, w_up, preferred_element_type=f32)]
    unnamed x132 -> x136, local copies, waits for them, and re-layouts: 102 us -> 19.7 us
    unnamed x17 -> x0, waiting for transfers between devices: 72.6 us -> none
    psum x1 -> x0, blocking collectives: 53.5 us -> none  [local(): total_squares = lax.psum(squares, ('batch', 'mp'))]
  transfers between devices with their start and end apart: 15 -> 0, of which waited for: 14 -> 0; matrix products, arithmetic and copies ran while one was open for 8% -> 0% of each run, Pallas kernels for 0% -> 0%
where the time goes in v1:
time: 432 us; the launch traced here: 425 us
  Pallas kernels  302 us (70%)
  matrix products  57.1 us (13%)
  local copies, waits for them, and re-layouts  36.2 us (8%)
  other arithmetic  23.6 us (5%)
  between operations  5.49 us (1%)
    pallas_call x4, Pallas kernels, call(): pl.pallas_call(kernel, in_specs=in_specs or [on_chip] * len(arguments), o...  260 us
    pallas_call x1, Pallas kernels, update_table(): pl.pallas_call(partial(table_kernel, rate), grid=(height // block,), in_s...  27.7 us
    unnamed x136, local copies, waits for them, and re-layouts  19.7 us
    dot_general x1, matrix products, local(): up = jnp.einsum('td,zdf->ztf', hidden_low, w_up, preferred_element_type=f32)  13.5 us
    dot_general x4, matrix products, dot(): lax.dot_general(left, right, ((left_dims, right_dims), ((), ())), preferr...  9.6 us
    dot_general x1, matrix products, local(): jnp.einsum('tn,znf->ztf', grad_mlp_low, w_down, preferred_element_type=f32)  9 us

profile of v1, /device:TPU:0, one launch (start us, length us, event | category | flops | bytes accessed | tf_op | source)
XLA Modules:
  0.0 424.6 jit_solution(4118548192106957868)
XLA Ops:
  3.6 3.6 gather_fusion
  7.8 12.5 %shard_map.365 = s32[32,2,384]{2,1,0:T(2,128)} custom-call(s32[2,384]{1,0:T(2,128)} %pad_add_fusion.x_ref), custom_call_target="tpu_custom_call" | custom-call | tf_op jit(solution)/shard_map/pallas_call | solution.py:204
  20.3 1.2 slice_reduce_fusion.3
  25.3 1.1 select_reduce_fusion.3
  27.1 1.9 fusion.63
  30.4 2.8 multiply_sine_fusion
  33.2 1.6 pad_maximum_fusion.cos_ref
  34.9 1.6 pad_maximum_fusion.1.sin_ref
  37.4 6.9 %shard_map.366 = bf16[288,768]{1,0:T(8,128)(2,1)} custom-call(s32[288]{0:T(512)} %max.24.list_ref, f32[3816,768]{1,0:T(8,128)} %get-tuple-element.1796), custom_call_target="tpu_custom_call" | custom-call | tf_op jit(solution)/shard_map/pallas_call | solution.py:1585
  44.4 1.2 copy.250.segq_ref.segk_ref
  47.5 1.0 convert_element_type.157
  48.6 0.8 copy.251.refs_0_
  49.4 1.6 convert_bitcast_fusion.refs_4_
  51.0 93.3 %shard_map.367 = (bf16[4,2,2,2,96,576]{5,4,3,2,1,0:T(8,128)(2,1)}, bf16[4,2,2,2,96,256]{5,4,3,2,1,0:T(8,128)(2,1)}, bf16[4,2,2,2,96,768]{5,4,3,2,1,0:T(8,128)(2,...) custom-call(bf16[2,144,768]{2,1,0:T(8,128)(2,1)} %bitcast.237, ...), custom_call_target="tpu_custom_call" | custom-call | tf_op jit(solution)/shard_map/pallas_call | solution.py:204
  144.3 2.7 fusion.126
  147.3 1.2 slice_convert_fusion
  148.9 4.8 %fusion.128 = f32[4,768,384]{2,1,0:T(8,128)S(1)} fusion(bf16[4,768,768]{2,1,0:T(8,128)(2,1)} %bitcast.262, bf16[384,768,1]{1,0,2:T(8,128)(2,1)S(1)} %fusion.59), kind=kOutput, calls=%fused_computation.290 | convolution fusion | flops 1811939328 | bytes 10027008 | tf_op jit(solution)/shard_map/td,zdf->ztf/dot_general | solution.py:1832
  153.8 13.5 %fusion.38 = (bf16[4,384,768]{1,2,0:T(8,128)(2,1)S(1)}, f32[4,768,384]{2,1,0:T(8,128)}) fusion(f32[4,768,384]{2,1,0:T(8,128)S(1)} %fusion.128, bf16[4,768,768]{2,1,0:T(8,128)(2,1)S(1)} %bitcast.258, bf16[384,768,1]{1,0,2:T(8,128)(2,1)S(1)} %fusion.59), kind=kOutput, calls=%fused_computation.76 | convolution fusion | flops 1819017216 | bytes 17104896 | tf_op jit(solution)/shard_map/td,zdf->ztf/dot_general | solution.py:1833
  167.3 2.2 fusion.127
  169.9 0.8 copy-done.16
  171.9 18.2 %shard_map.368 = (f32[8,128]{1,0:T(8,128)S(1)}, f32[384,768]{1,0:T(8,128)S(1)}) custom-call(s32[1]{0:T(128)S(6)} %copy.345.queries_ref, f32[384,768]{1,0:T(8,128)S(1)} %multiply_multiply_fusion.hidden_ref, s32[1,384]{1,0:T(1,128)S(1)} %dynamic_slice.84.seg_ref, f32[64,1]{1,0:T(8,128)S(1)} %reshape.1238.counts_ref), custom_call_target="tpu_custom_call" | custom-call | tf_op jit(solution)/shard_map/pallas_call | solution.py:204
  191.2 1.7 copy-done.45
  192.9 9.0 %fusion.37 = (bf16[4,384,768]{1,2,0:T(8,128)(2,1)S(1)}, bf16[4,384,768]{1,2,0:T(8,128)(2,1)S(1)}) fusion(f32[4,768,384]{2,1,0:T(8,128)S(1)} %copy-done.45, f32[4,768,384]{2,1,0:T(8,128)} %get-tuple-element.1321, bf16[4,768,768]{2,1,0:T(8,128)(2,1)} %bitcast.266, f32[384,768]{1,0:T(8,128)S(1)} %get-tuple-element.1280, f32[384]{0:T(512)S(1)} %negate_multiply_fusion.1), kind=kOutput, calls=%fused_computation.74 | convolution fusion | flops 1829044224 | bytes 20055552 | tf_op jit(solution)/shard_map/tn,znf->ztf/dot_general | solution.py:1847
  202.0 2.3 fusion.46
  204.3 2.4 multiply_reduce_fusion.1
  207.4 1.0 copy-done.29
  208.4 0.8 fusion.44
  209.6 1.6 copy.272
  211.2 7.0 %convolution_convert_fusion = bf16[4,768,768]{1,2,0:T(8,128)(2,1)} fusion(bf16[4,384,768]{1,2,0:T(8,128)(2,1)} %copy-done.46, f32[384,768]{1,0:T(8,128)} %copy-done.28, f32[384]{0:T(512)S(1)} %negate_multiply_fusion.1), kind=kOutput, calls=%fused_computation.83 | convolution fusion | flops 1814888448 | bytes 8259072 | tf_op jit(solution)/shard_map/tn,ztf->znf/dot_general | solution.py:1848
  218.3 4.8 %convolution_convert_fusion.1 = bf16[4,768,768]{1,2,0:T(8,128)(2,1)} fusion(bf16[4,384,768]{1,2,0:T(8,128)(2,1)S(1)} %copy-done.50, bf16[384,768,1]{1,0,2:T(8,128)(2,1)S(1)} %fusion.59), kind=kOutput, calls=%fused_computation.84 | convolution fusion | flops 1814298624 | bytes 7667712 | tf_op jit(solution)/shard_map/td,ztf->zdf/dot_general | solution.py:1856
  223.1 4.8 %convolution_convert_fusion.2 = bf16[4,768,768]{1,2,0:T(8,128)(2,1)} fusion(bf16[4,384,768]{1,2,0:T(8,128)(2,1)S(1)} %copy-done.48, bf16[384,768,1]{1,0,2:T(8,128)(2,1)S(1)} %fusion.59), kind=kOutput, calls=%fused_computation.85 | convolution fusion | flops 1814298624 | bytes 7667712 | tf_op jit(solution)/shard_map/td,ztf->zdf/dot_general | solution.py:1855
  228.0 1.9 copy.307
  229.9 2.1 fusion.66
  232.1 1.2 copy.262
  234.0 0.9 select_reduce_fusion.4
  234.9 1.1 broadcast_in_dim_reshape.9.listq_ref
  236.6 136.0 %shard_map.370 = (f32[96,768]{1,0:T(8,128)}, f32[96,768]{1,0:T(8,128)}, f32[96,768]{1,0:T(8,128)}, f32[96,256]{1,0:T(8,128)}, f32[96,576]{1,0:T(8,128)}, /*index...) custom-call(bf16[4,384,192]{2,1,0:T(8,128)(2,1)} %bitcast.232, ...), custom_call_target="tpu_custom_call" | custom-call | tf_op jit(solution)/shard_map/pallas_call | solution.py:204
  375.0 0.9 copy.278.refs_0_
  376.0 2.0 copy.279.refs_1_
  378.1 1.9 copy.280.refs_2_
  380.0 0.9 copy.281.refs_9_
  380.9 0.9 copy.282.refs_10_
  381.8 0.9 copy.283.refs_11_
  382.8 7.1 %shard_map.372 = (f32[96,3,192]{2,1,0:T(4,128)S(1)}, f32[96,3,192]{2,1,0:T(4,128)S(1)}, f32[96,3,192]{2,1,0:T(4,128)S(1)}, f32[192,96]{1,0:T(8,128)}, f32[192,96...) custom-call(f32[1]{0:T(128)} %bitcast.61.scale_ref, ...), custom_call_target="tpu_custom_call" | custom-call | tf_op jit(solution)/shard_map/pallas_call | solution.py:1663
  390.7 0.9 copy.285
  392.3 0.9 copy.287
  394.0 0.9 copy.289
  394.8 27.7 %shard_map.371 = (f32[3816,768]{1,0:T(8,128)}, f32[3816,768]{1,0:T(8,128)}, f32[3816,768]{1,0:T(8,128)}) custom-call(s32[1]{0:T(128)} %bitcast.60.rounds_ref, f32[1]{0:T(128)} %bitcast.61.scale_ref, s32[11,1152]{1,0:T(8,128)} %copy-done.25, bf16[1152,768]{1,0:T(8,128)(2,1)S(1)} %copy-done.24, bf16[10,1152,768]{2,1,0:T(8,128)(2,1)} %get-tuple-element.883.more_ref, ...), custom_call_target="tpu_custom_call" | custom-call | tf_op jit(solution)/shard_map/pallas_call | solution.py:1627
  (219 shorter events, 21.1 us)
Async XLA Ops:
  0.7 6.5 %copy-start = (s32[1,1536]{1,0:T(1,128)S(1)}, s32[1,1536]{1,0:T(1,128)}, u32[]{:S(2)}) copy-start(s32[1,1536]{1,0:T(1,128)} %param.31) | copy-start | bytes 18436
  22.8 3.8 copy-start.20
  22.9 211.1 %copy-start.21 = (s32[8,1536]{1,0:T(8,128)}, s32[8,1536]{1,0:T(8,128)S(1)}, u32[]{:S(2)}) copy-start(s32[8,1536]{1,0:T(8,128)S(1)} %get-tuple-element.1691) | copy-start | bytes 147460
  24.7 4.2 copy-start.38
  24.7 4.2 copy-start.40
  24.7 19.7 %copy-start.37 = (s32[1,1536]{1,0:T(1,128)}, s32[1,1536]{1,0:T(1,128)S(1)}, u32[]{:S(2)}) copy-start(s32[1,1536]{1,0:T(1,128)S(1)} %get-tuple-element.1326.segk_ref.segq_ref) | copy-start | bytes 18436
  30.0 6.5 %copy-start.30 = (s32[1536,1]{0,1:T(1,128)}, s32[1536,1]{0,1:T(1,128)S(1)}, u32[]{:S(2)}) copy-start(s32[1536,1]{0,1:T(1,128)S(1)} %get-tuple-element.1805) | copy-start | bytes 18436
  30.0 6.4 %copy-start.32 = (s32[1536,1]{0,1:T(1,128)}, s32[1536,1]{0,1:T(1,128)S(1)}, u32[]{:S(2)}) copy-start(s32[1536,1]{0,1:T(1,128)S(1)} %get-tuple-element.1806) | copy-start | bytes 18436
  37.4 8.2 %copy-start.22 = (f32[96,2,768]{2,1,0:T(2,128)S(1)}, f32[96,2,768]{2,1,0:T(2,128)}, u32[]{:S(2)}) copy-start(f32[96,2,768]{2,1,0:T(2,128)} %refs_6_.1) | copy-start | bytes 1769476
  44.4 2.2 copy-start.11
  46.5 97.8 %copy-start.42 = (bf16[256]{0:T(256)(128)(2,1)}, bf16[256]{0:T(256)(128)(2,1)S(1)}, u32[]{:S(2)}) copy-start(bf16[256]{0:T(256)(128)(2,1)S(1)} %pad.9.clone) | copy-start | bytes 1540
  147.0 20.2 %copy-start.18 = (f32[384,768]{1,0:T(8,128)}, f32[384,768]{1,0:T(8,128)S(1)}, u32[]{:S(2)}) copy-start(f32[384,768]{1,0:T(8,128)S(1)} %get-tuple-element.1319) | copy-start | bytes 3538948
  148.7 5.1 %slice-start = ((s8[4718592]{0:T(1024)(128)(4,1)}), s8[4194304]{0:T(1024)(128)(4,1)S(1)}, s32[]{:S(2)}) async-start(s8[4718592]{0:T(1024)(128)(4,1)} %bitcast.256), calls=%async_computation | async-start | bytes 8388608
  148.9 4.8 %slice-start.1 = ((s8[4718592]{0:T(1024)(128)(4,1)}), s8[524288]{0:T(1024)(128)(4,1)S(1)}, s32[]{:S(2)}) async-start(s8[4718592]{0:T(1024)(128)(4,1)} %bitcast.256), calls=%async_computation.1 | async-start | bytes 1048576
  148.9 18.3 %slice-start.6 = ((s8[4718592]{0:T(1024)(128)(4,1)}), s8[4194304]{0:T(1024)(128)(4,1)S(1)}, s32[]{:S(2)}) async-start(s8[4718592]{0:T(1024)(128)(4,1)} %bitcast.267), calls=%async_computation.6 | async-start | bytes 8388608
  153.7 13.5 %copy-start.44 = (f32[4,768,384]{2,1,0:T(8,128)}, f32[4,768,384]{2,1,0:T(8,128)S(1)}, u32[]{:S(2)}) copy-start(f32[4,768,384]{2,1,0:T(8,128)S(1)} %fusion.128) | copy-start | bytes 14155780
  153.8 13.5 %slice-start.7 = ((s8[4718592]{0:T(1024)(128)(4,1)}), s8[524288]{0:T(1024)(128)(4,1)S(1)}, s32[]{:S(2)}) async-start(s8[4718592]{0:T(1024)(128)(4,1)} %bitcast.267), calls=%async_computation.7 | async-start | bytes 1048576
  167.3 2.3 copy-start.46
  171.2 19.0 %copy-start.17 = (f32[384,768]{1,0:T(8,128)S(1)}, f32[384,768]{1,0:T(8,128)}, u32[]{:S(2)}) copy-start(f32[384,768]{1,0:T(8,128)} %copy-done.16) | copy-start | bytes 3538948
  190.1 2.8 copy-start.45
  190.7 11.3 %slice-start.4 = ((s8[4718592]{0:T(1024)(128)(4,1)}), s8[4194304]{0:T(1024)(128)(4,1)S(1)}, s32[]{:S(2)}) async-start(s8[4718592]{0:T(1024)(128)(4,1)} %bitcast.263), calls=%async_computation.4 | async-start | bytes 8388608
  190.7 13.6 %slice-start.2 = ((s8[4718592]{0:T(1024)(128)(4,1)}), s8[4194304]{0:T(1024)(128)(4,1)S(1)}, s32[]{:S(2)}) async-start(s8[4718592]{0:T(1024)(128)(4,1)} %bitcast.259), calls=%async_computation.2 | async-start | bytes 8388608
  191.2 10.7 %copy-start.28 = (f32[384,768]{1,0:T(8,128)}, f32[384,768]{1,0:T(8,128)S(1)}, u32[]{:S(2)}) copy-start(f32[384,768]{1,0:T(8,128)S(1)} %get-tuple-element.1280) | copy-start | bytes 3538948
  192.9 9.1 %slice-start.5 = ((s8[4718592]{0:T(1024)(128)(4,1)}), s8[524288]{0:T(1024)(128)(4,1)S(1)}, s32[]{:S(2)}) async-start(s8[4718592]{0:T(1024)(128)(4,1)} %bitcast.263), calls=%async_computation.5 | async-start | bytes 1048576
  192.9 11.4 %slice-start.3 = ((s8[4718592]{0:T(1024)(128)(4,1)}), s8[524288]{0:T(1024)(128)(4,1)S(1)}, s32[]{:S(2)}) async-start(s8[4718592]{0:T(1024)(128)(4,1)} %bitcast.259), calls=%async_computation.3 | async-start | bytes 1048576
  201.9 2.4 copy-start.47
  201.9 2.4 copy-start.49
  202.0 2.4 copy-start.19
  208.4 21.5 %copy-start.15 = (f32[384,768]{1,0:T(8,128)}, f32[384,768]{1,0:T(8,128)S(1)}, u32[]{:S(2)}) copy-start(f32[384,768]{1,0:T(8,128)S(1)} %broadcast_add_fusion.3.first_ref) | copy-start | bytes 3538948
  211.2 7.0 %copy-start.50 = (bf16[4,384,768]{1,2,0:T(8,128)(2,1)S(1)}, bf16[4,384,768]{1,2,0:T(8,128)(2,1)}, u32[]{:S(2)}) copy-start(bf16[4,384,768]{1,2,0:T(8,128)(2,1)} %copy-done.49) | copy-start | bytes 7077892
  218.3 4.8 %copy-start.48 = (bf16[4,384,768]{1,2,0:T(8,128)(2,1)S(1)}, bf16[4,384,768]{1,2,0:T(8,128)(2,1)}, u32[]{:S(2)}) copy-start(bf16[4,384,768]{1,2,0:T(8,128)(2,1)} %copy-done.47) | copy-start | bytes 7077892
  223.1 4.9 %copy-start.23 = (bf16[4,2,2,2,96,256]{5,4,3,2,1,0:T(8,128)(2,1)S(1)}, bf16[4,2,2,2,96,256]{5,4,3,2,1,0:T(8,128)(2,1)}, u32[]{:S(2)}) copy-start(bf16[4,2,2,2,96,256]{5,4,3,2,1,0:T(8,128)(2,1)} %get-tuple-element.868) | copy-start | bytes 4718596
  373.7 6.3 %copy-start.27 = (f32[768,96]{0,1:T(8,128)S(1)}, f32[768,96]{0,1:T(8,128)}, u32[]{:S(2)}) copy-start(f32[768,96]{0,1:T(8,128)} %param.38) | copy-start | bytes 884740
  373.7 7.2 %copy-start.34 = (f32[768,96]{0,1:T(8,128)S(1)}, f32[768,96]{0,1:T(8,128)}, u32[]{:S(2)}) copy-start(f32[768,96]{0,1:T(8,128)} %param.44) | copy-start | bytes 884740
  373.7 8.1 %copy-start.35 = (f32[768,96]{0,1:T(8,128)S(1)}, f32[768,96]{0,1:T(8,128)}, u32[]{:S(2)}) copy-start(f32[768,96]{0,1:T(8,128)} %param.50) | copy-start | bytes 884740
  375.9 6.8 %copy-start.3 = (f32[192,96]{1,0:T(8,128)S(1)}, f32[192,96]{1,0:T(8,128)}, u32[]{:S(2)}) copy-start(f32[192,96]{1,0:T(8,128)} %refs_3_.1) | copy-start | bytes 221188
  375.9 6.8 %copy-start.4 = (f32[96,768]{1,0:T(8,128)S(1)}, f32[96,768]{1,0:T(8,128)}, u32[]{:S(2)}) copy-start(f32[96,768]{1,0:T(8,128)} %get-tuple-element.887.gate_ref) | copy-start | bytes 884740
  376.0 6.8 %copy-start.5 = (f32[96,768]{1,0:T(8,128)S(1)}, f32[96,768]{1,0:T(8,128)}, u32[]{:S(2)}) copy-start(f32[96,768]{1,0:T(8,128)} %get-tuple-element.888.up_ref) | copy-start | bytes 884740
  376.0 6.8 %copy-start.6 = (f32[96,768]{1,0:T(8,128)S(1)}, f32[96,768]{1,0:T(8,128)}, u32[]{:S(2)}) copy-start(f32[96,768]{1,0:T(8,128)} %get-tuple-element.889.down_ref) | copy-start | bytes 884740
  376.0 6.8 %copy-start.7 = (f32[96,576]{1,0:T(8,128)S(1)}, f32[96,576]{1,0:T(8,128)}, u32[]{:S(2)}) copy-start(f32[96,576]{1,0:T(8,128)} %get-tuple-element.885.qkv_ref) | copy-start | bytes 663556
  376.0 6.8 %copy-start.8 = (f32[192,96]{1,0:T(8,128)S(1)}, f32[192,96]{1,0:T(8,128)}, u32[]{:S(2)}) copy-start(f32[192,96]{1,0:T(8,128)} %refs_4_.1) | copy-start | bytes 221188
  376.0 6.8 %copy-start.9 = (f32[192,96]{1,0:T(8,128)S(1)}, f32[192,96]{1,0:T(8,128)}, u32[]{:S(2)}) copy-start(f32[192,96]{1,0:T(8,128)} %refs_5_.1) | copy-start | bytes 221188
  376.0 6.8 %copy-start.10 = (f32[96,256]{1,0:T(8,128)S(1)}, f32[96,256]{1,0:T(8,128)}, u32[]{:S(2)}) copy-start(f32[96,256]{1,0:T(8,128)} %get-tuple-element.886.misc_ref) | copy-start | bytes 294916
  376.0 6.8 %copy-start.12 = (f32[2,96]{1,0:T(2,128)S(1)}, f32[2,96]{1,0:T(2,128)}, u32[]{:S(2)}) copy-start(f32[2,96]{1,0:T(2,128)} %refs_12_.1) | copy-start | bytes 2308
  376.0 6.8 %copy-start.13 = (f32[2,96]{1,0:T(2,128)S(1)}, f32[2,96]{1,0:T(2,128)}, u32[]{:S(2)}) copy-start(f32[2,96]{1,0:T(2,128)} %refs_13_.1) | copy-start | bytes 2308
  376.0 6.8 %copy-start.14 = (f32[2,96]{1,0:T(2,128)S(1)}, f32[2,96]{1,0:T(2,128)}, u32[]{:S(2)}) copy-start(f32[2,96]{1,0:T(2,128)} %refs_14_.1) | copy-start | bytes 2308
  391.6 3.3 copy-start.24
  394.8 28.2 %copy-start.1 = (s32[1,1536]{1,0:T(1,128)S(1)}, s32[1,1536]{1,0:T(1,128)}, u32[]{:S(2)}) copy-start(s32[1,1536]{1,0:T(1,128)} %param.31) | copy-start | bytes 18436
  (11 other events, 14.1 us)
